TPU v7x, 128 devices: a whole 4x4x4 slice. The times are simulated.
128 devices in a mesh: plane: 2 (over x_hi), slab: 64 (over x_lo, y, z, core).
Axes of the slice: x: 4 (x_hi: 2, x_lo: 2; x = x_hi * 2 + x_lo), y: 4, z: 4, core: 2. Of those that a mesh axis runs over, the one named last changes fastest.
Arguments:
- kappa: float32 [2, 4096, 4096], P('plane', 'slab'), may hold values from -2.5 to 2.5
- ray_offsets: float32 [2, 64, 2, 8, 4096], P(None, 'slab', 'plane'), may hold values from -0.5 to 0.5
Outputs:
- deflection: float32 [2, 64, 2, 8, 4096], P(None, 'slab', 'plane')
- jacobian: float32 [4, 64, 2, 8, 4096], P(None, 'slab', 'plane')
All inputs are finite; a program needn't handle non-finite values.
Results may differ from a plain program's by a relative error of at most 0.0003.
Values sent between devices are 32-bit elements; how exact they have to be, the bound alone decides.
No kernel may reach another device: no remote copies, remote signals or barrier semaphores. Data moves between devices by JAX's collectives and lax.ppermute only.
A program may use at most 64 MiB of HBM per device.

v0:
```python
import math

import jax
import jax.numpy as jnp
from jax import lax
from jax.sharding import PartitionSpec as P

STEP = 4
MARGIN = 8
PATCH_ROWS = 16
BLOCK = 64


lens_ratio = 0.5
screen_modes = 4.0


def padded_2(shard, sides, width):
    for axis, dim in sides:
        size, length = (lax.axis_size(axis), shard.shape[dim])
        up = [(i, (i + 1) % size) for i in range(size)]
        down = [(j, i) for i, j in up]
        last = lax.slice_in_dim(shard, length - width, length, axis=dim)
        initial = lax.slice_in_dim(shard, 0, width, axis=dim)
        before = lax.ppermute(last, axis, up)
        after = lax.ppermute(initial, axis, down)
        shard = jnp.concatenate([before, shard, after], axis=dim)
    return shard


def factor_pair(length):
    outer = 1
    trial = 1
    while trial * trial <= length:
        if length % trial == 0:
            outer = trial
        trial = trial + 1
    return (outer, length // outer)


def cos_sin(left_ids, right_ids, length):
    angles = (left_ids[:, None] * right_ids[None, :] % length).astype(jnp.float32) * (
        2.0 * math.pi / length
    )
    return (jnp.cos(angles), jnp.sin(angles))


def contract_first(values, table):
    return jnp.einsum("...ab,ak->...kb", values, table, precision=lax.Precision.HIGHEST)


def contract_second(values, table):
    return jnp.einsum("...kb,bm->...mk", values, table, precision=lax.Precision.HIGHEST)


def transform_last(real_part, imag_part, sign):
    length = real_part.shape[-1]
    outer, inner = factor_pair(length)
    leading = real_part.shape[:-1]
    outer_ids = jnp.arange(outer, dtype=jnp.int32)
    inner_ids = jnp.arange(inner, dtype=jnp.int32)
    cos_outer, sin_outer = cos_sin(outer_ids, outer_ids, outer)
    cos_twist, sin_twist = cos_sin(outer_ids, inner_ids, length)
    cos_inner, sin_inner = cos_sin(inner_ids, inner_ids, inner)
    split_real = real_part.reshape(leading + (outer, inner))
    section_real = contract_first(split_real, cos_outer)
    section_imag = sign * contract_first(split_real, sin_outer)
    if imag_part is not None:
        split_imag = imag_part.reshape(leading + (outer, inner))
        section_real = section_real - sign * contract_first(split_imag, sin_outer)
        section_imag = section_imag + contract_first(split_imag, cos_outer)
    twist_real = section_real * cos_twist - sign * section_imag * sin_twist
    twist_imag = sign * section_real * sin_twist + section_imag * cos_twist
    final_real = contract_second(twist_real, cos_inner) - sign * contract_second(
        twist_imag, sin_inner
    )
    final_imag = sign * contract_second(twist_real, sin_inner) + contract_second(
        twist_imag, cos_inner
    )
    return (final_real.reshape(leading + (length,)), final_imag.reshape(leading + (length,)))


def wavenumbers(indices, length):
    folded = jnp.minimum(indices, length - indices).astype(jnp.float32)
    return 2.0 * math.pi / length * folded


def spline_terms(offset):
    magnitude = jnp.abs(offset)
    inside = magnitude < 1.0
    remain = jnp.maximum(2.0 - magnitude, 0.0)
    weights = jnp.where(
        inside,
        2.0 / 3.0 - magnitude * magnitude + 0.5 * magnitude * magnitude * magnitude,
        remain * remain * remain / 6.0,
    )
    slopes = jnp.sign(offset) * jnp.where(
        inside, -2.0 * magnitude + 1.5 * magnitude * magnitude, -0.5 * remain * remain
    )
    curves = jnp.where(inside, 3.0 * magnitude - 2.0, remain)
    return (weights, slopes, curves)


def lens_fields(plane_blocks, ycoord, xcoord):
    column_ids = jnp.arange(plane_blocks.shape[2]).astype(xcoord.dtype)
    row_ids = jnp.arange(plane_blocks.shape[0]).astype(ycoord.dtype)
    x_weights = jnp.stack(spline_terms(xcoord[:, :, None] - column_ids), axis=1)
    across = jnp.einsum("pbc,bkrc->bkpr", plane_blocks, x_weights, precision=lax.Precision.HIGHEST)
    down_weights, down_slopes, down_curves = spline_terms(ycoord[:, None, :] - row_ids[:, None])
    slope_down = jnp.sum(down_slopes * across[:, 0], axis=1)
    slope_across = jnp.sum(down_weights * across[:, 1], axis=1)
    bend_down = jnp.sum(down_curves * across[:, 0], axis=1)
    bend_across = jnp.sum(down_weights * across[:, 2], axis=1)
    bend_mixed = jnp.sum(down_slopes * across[:, 1], axis=1)
    return (slope_down, slope_across, bend_down, bend_across, bend_mixed)


def ray_row_outputs(window, shift_y, shift_x):
    grid_width = shift_y.shape[0]
    block_count = grid_width // BLOCK
    column_view = window.reshape(window.shape[0], PATCH_ROWS, block_count + 1, BLOCK)
    blocks = jnp.concatenate([column_view[:, :, :-1], column_view[:, :, 1:]], axis=3)
    centre_row = PATCH_ROWS // 2 - 1
    ycoord = centre_row + STEP * shift_y.reshape(block_count, BLOCK)
    xcoord = (
        BLOCK // 2 + jnp.arange(BLOCK).astype(shift_x.dtype) + shift_x.reshape(block_count, BLOCK)
    )
    first = lens_fields(blocks[0], ycoord, xcoord)
    second = lens_fields(blocks[1], ycoord - lens_ratio * first[0], xcoord - lens_ratio * first[1])
    hess_yy, hess_xx, hess_xy = (first[2], first[3], first[4])
    other_yy, other_xx, other_xy = (second[2], second[3], second[4])
    lensed_yy = 1.0 - lens_ratio * hess_yy
    lensed_xx = 1.0 - lens_ratio * hess_xx
    lensed_xy = -lens_ratio * hess_xy
    entry_yy = 1.0 - hess_yy - (other_yy * lensed_yy + other_xy * lensed_xy)
    entry_yx = -hess_xy - (other_yy * lensed_xy + other_xy * lensed_xx)
    entry_xy = -hess_xy - (other_xy * lensed_yy + other_xx * lensed_xy)
    entry_xx = 1.0 - hess_xx - (other_xy * lensed_xy + other_xx * lensed_xx)
    deflect = jnp.stack([first[0] + second[0], first[1] + second[1]]).reshape(2, grid_width)
    jacob = jnp.stack([entry_yy, entry_yx, entry_xy, entry_xx]).reshape(4, grid_width)
    return (deflect, jacob)


def on_device(kappa, ray_offsets):
    row_count = kappa.shape[1]
    grid_width = kappa.shape[2]
    slab_count = lax.axis_size("slab")
    half_rows = row_count // 2
    strip_rows = half_rows + 2 * MARGIN

    def to_local(values):
        return jnp.transpose(values.reshape(row_count, slab_count, row_count), (2, 1, 0)).reshape(
            row_count, grid_width
        )

    row_real, row_imag = transform_last(kappa[0], None, -1.0)
    recv_real, recv_imag = (
        lax.all_to_all(row_real, "slab", split_axis=1, concat_axis=1, tiled=True),
        lax.all_to_all(row_imag, "slab", split_axis=1, concat_axis=1, tiled=True),
    )
    spec_real, spec_imag = transform_last(to_local(recv_real), to_local(recv_imag), -1.0)
    first_wave = lax.axis_index("slab") * row_count
    wave_ids = jnp.arange(grid_width, dtype=jnp.int32)
    mine_ids = first_wave + jnp.arange(row_count, dtype=jnp.int32)
    wave_all = wavenumbers(wave_ids, grid_width)
    wave_mine = wavenumbers(mine_ids, grid_width)
    screen = (2.0 * math.pi * screen_modes / grid_width) ** 2
    denom = wave_mine[:, None] ** 2 + wave_all[None, :] ** 2 + screen
    anchor = (mine_ids[:, None] == 0) & (wave_ids[None, :] == 0)
    screened = jnp.where(anchor, 0.0, -2.0 / (denom * float(grid_width * grid_width)))
    inv_real, inv_imag = transform_last(spec_real * screened, spec_imag * screened, 1.0)
    back_real, back_imag = (
        lax.all_to_all(inv_real, "slab", split_axis=1, concat_axis=1, tiled=True),
        lax.all_to_all(inv_imag, "slab", split_axis=1, concat_axis=1, tiled=True),
    )
    potential = transform_last(to_local(back_real), to_local(back_imag), 1.0)[0]
    together = lax.all_gather(potential[None], "plane", axis=0, tiled=True)
    rimmed = padded_2(together, (("slab", 1),), MARGIN)
    strips = lax.dynamic_slice_in_dim(rimmed, lax.axis_index("plane") * half_rows, strip_rows, 1)
    padded = jnp.concatenate(
        [strips[:, :, grid_width - BLOCK // 2 :], strips, strips[:, :, : BLOCK // 2]], axis=2
    )
    ray_count = ray_offsets.shape[3]
    centre_row = PATCH_ROWS // 2 - 1
    row_shifts = ray_offsets[0, 0, 0]
    column_shifts = ray_offsets[1, 0, 0]

    def one_row(ray_row):
        first_row = STEP * ray_row + (STEP // 2 - centre_row + MARGIN)
        window = lax.dynamic_slice_in_dim(padded, first_row, PATCH_ROWS, 1)
        shift_y = lax.dynamic_index_in_dim(row_shifts, ray_row, 0, keepdims=False)
        shift_x = lax.dynamic_index_in_dim(column_shifts, ray_row, 0, keepdims=False)
        return ray_row_outputs(window, shift_y, shift_x)

    deflect, jacob = lax.map(one_row, jnp.arange(ray_count, dtype=jnp.int32))
    deflection = jnp.transpose(deflect, (1, 0, 2))[:, None, None]
    jacobian = jnp.transpose(jacob, (1, 0, 2))[:, None, None]
    return (deflection, jacobian)


def solution(mesh):
    placed = (P("plane", "slab", None), P(None, "slab", "plane", None, None))
    return jax.shard_map(
        on_device,
        mesh=mesh,
        in_specs=placed,
        out_specs=(P(None, "slab", "plane", None, None), P(None, "slab", "plane", None, None)),
        check_vma=False,
    )
```

profile of v0, /device:TPU:1, one launch (start us, length us, event | category | flops | bytes accessed | tf_op | source)
XLA Modules:
  0.0 723.7 jit_solution(14605992156972136415)
XLA Ops:
  10.4 3.7 fusion.203
  18.4 8.0 %fusion.138 = f32[64,64,64]{2,0,1:T(8,128)S(1)} fusion(f32[64,64,64]{2,0,1:T(8,128)S(1)} %fusion.203, f32[64,64,64]{2,0,1:T(8,128)} %fusion.219, f32[64,64]{1,0:T(8,128)S(1)} %copy.52, f32[64,64]{1,0:T(8,128)S(1)} %copy.51), kind=kOutput, calls=%fused_computation.191 | convolution fusion | flops 202170368 | bytes 3178496 | tf_op jit(solution)/shard_map/...kb,bm->...mk/dot_general | solution.py:53
  26.4 6.6 add_bitcast_fusion.1
  38.9 10.9 %all-to-all-start.1 = ((f32[64,1,4096]{2,1,0:T(1,128)}), f32[64,1,4096]{2,1,0:T(1,128)S(1)}, u32[]{:S(2)}, u32[]{:S(2)}) async-start(f32[64,1,4096]{2,1,0:T(1,128)} %reshape.785), calls=%async_computation.1 | async-start | bytes 2097152 | tf_op jit(solution)/shard_map/all_to_all | solution.py:159
  49.9 8.0 %fusion.140 = f32[64,64,64]{2,0,1:T(8,128)S(1)} fusion(f32[64,64,64]{2,0,1:T(8,128)S(1)} %fusion.203, f32[64,64,64]{2,0,1:T(8,128)} %fusion.219, f32[64,64]{1,0:T(8,128)S(1)} %copy.52, f32[64,64]{1,0:T(8,128)S(1)} %copy.51), kind=kOutput, calls=%fused_computation.193 | convolution fusion | flops 202170368 | bytes 3178496 | tf_op jit(solution)/shard_map/...kb,bm->...mk/dot_general | solution.py:53
  57.8 6.2 subtract_bitcast_fusion.2
  67.6 9.5 %all-to-all-start = ((f32[64,1,4096]{2,1,0:T(1,128)}), f32[64,1,4096]{2,1,0:T(1,128)}, u32[]{:S(2)}, u32[]{:S(2)}) async-start(f32[64,1,4096]{2,1,0:T(1,128)} %reshape.787), calls=%async_computation | async-start | bytes 2097152 | tf_op jit(solution)/shard_map/all_to_all | solution.py:158
  94.0 4.4 reduce.9
  104.0 3.9 multiply_subtract_fusion.6
  110.3 6.2 fusion.122
  116.5 6.2 fusion.124
  122.7 6.5 bitcast_multiply_fusion.1
  133.4 6.7 bitcast_multiply_fusion
  144.6 6.2 fusion.114
  150.8 6.2 add_bitcast_fusion
  163.2 8.1 %all-to-all-start.3 = ((f32[64,1,4096]{2,1,0:T(1,128)}), f32[64,1,4096]{2,1,0:T(1,128)S(1)}, u32[]{:S(2)}, u32[]{:S(2)}) async-start(f32[64,1,4096]{2,1,0:T(1,128)} %reshape.789), calls=%async_computation.3 | async-start | bytes 2097152 | tf_op jit(solution)/shard_map/all_to_all | solution.py:174
  171.3 7.9 %fusion.116 = f32[64,64,64]{2,0,1:T(8,128)S(1)} fusion(f32[64,64,64]{2,0,1:T(8,128)} %copy-done.6, f32[64,64,64]{2,0,1:T(8,128)S(1)} %convolution_subtract_fusion, f32[64,64]{1,0:T(8,128)S(1)} %copy.50, f32[64,64]{1,0:T(8,128)S(1)} %copy.49), kind=kOutput, calls=%fused_computation.167 | convolution fusion | flops 202170368 | bytes 3178496 | tf_op jit(solution)/shard_map/...kb,bm->...mk/dot_general | solution.py:53
  179.2 6.2 subtract_bitcast_fusion.1
  189.0 9.1 %all-to-all-start.2 = ((f32[64,1,4096]{2,1,0:T(1,128)}), f32[64,1,4096]{2,1,0:T(1,128)}, u32[]{:S(2)}, u32[]{:S(2)}) async-start(f32[64,1,4096]{2,1,0:T(1,128)} %reshape.791), calls=%async_computation.2 | async-start | bytes 2097152 | tf_op jit(solution)/shard_map/all_to_all | solution.py:173
  215.2 4.4 reduce.11
  225.0 4.0 fusion.168
  231.1 6.2 fusion.102
  237.3 6.3 subtract_bitcast_fusion
  245.3 36.8 %all-gather.2.cloned.1.call-done = f32[2,64,4096]{2,1,0:T(8,128)} async-done(((f32[1,64,4096]{2,1,0:T(8,128)}), f32[2,64,4096]{2,1,0:T(8,128)}) %all-gather.2.cloned.1.call-update) | async-done | bytes 2097168 | tf_op jit(solution)/shard_map/all_gather | solution.py:177
  294.5 421.9 %while.15 = (s32[]{:T(128)}, f32[8,2,4096]{2,0,1:T(8,128)}, f32[8,4,4096]{2,0,1:T(8,128)}, s32[8]{0:T(128)S(1)}, f32[8,4096]{1,0:T(8,128)S(1)}, /*index=5*/f32[8...) while((s32[]{:T(128)}, f32[8,2,4096]{2,0,1:T(8,128)}, ...), condition=%wide.region_11.12_spmd, body=%wide.region_0.11_spmd.sunk | while | flops 642666752 | bytes 60296028 | solution.py:195
  315.3 3.6 fusion.401
  325.2 14.3 %fusion.403 = f32[64,3,16,64]{3,2,1,0:T(8,128)} fusion(f32[64,1,64,128]{3,2,1,0:T(8,128)S(1)} %copy-done, f32[64,1,64,128]{3,2,1,0:T(8,128)S(1)} %copy-done.1, f32[64,1,64,128]{3,2,1,0:T(8,128)S(1)} %get-tuple-element.233, f32[2,16,64,64]{3,1,2,0:T(8,128)S(1)} %copy.94, f32[2,16,64,64]{3,1,2,0:T(8,128)S(1)} %copy.95), kind=kOutput, calls=%fused_computation.55.clone.1 | convolution fusion | flops 305266688 | bytes 8126464 | tf_op jit(solution)/shard_map/while/body/eval_jaxpr/pbc,bkrc->bkpr/dot_general | solution.py:108
  344.4 13.2 %fusion.406 = f32[64,3,16,64]{3,2,0,1:T(8,128)S(1)} fusion(f32[2,16,64,64]{3,1,2,0:T(8,128)S(1)} %copy-done.3, f32[2,16,64,64]{3,1,2,0:T(8,128)S(1)} %copy.94, f32[64,1,64,128]{3,2,1,0:T(8,128)S(1)} %get-tuple-element.238, f32[64,1,64,128]{3,2,1,0:T(8,128)S(1)} %get-tuple-element.239, f32[64,1,64,128]{3,2,1,0:T(8,128)S(1)} %get-tuple-element.240), kind=kOutput, calls=%fused_computation.56.clone.1 | convolution fusion | flops 305266688 | bytes 8126464 | tf_op jit(solution)/shard_map/while/body/eval_jaxpr/pbc,bkrc->bkpr/dot_general | solution.py:108
  365.7 3.6 fusion.401
  375.7 14.3 %fusion.403 = f32[64,3,16,64]{3,2,1,0:T(8,128)} fusion(f32[64,1,64,128]{3,2,1,0:T(8,128)S(1)} %copy-done, f32[64,1,64,128]{3,2,1,0:T(8,128)S(1)} %copy-done.1, f32[64,1,64,128]{3,2,1,0:T(8,128)S(1)} %get-tuple-element.233, f32[2,16,64,64]{3,1,2,0:T(8,128)S(1)} %copy.94, f32[2,16,64,64]{3,1,2,0:T(8,128)S(1)} %copy.95), kind=kOutput, calls=%fused_computation.55.clone.1 | convolution fusion | flops 305266688 | bytes 8126464 | tf_op jit(solution)/shard_map/while/body/eval_jaxpr/pbc,bkrc->bkpr/dot_general | solution.py:108
  394.9 13.2 %fusion.406 = f32[64,3,16,64]{3,2,0,1:T(8,128)S(1)} fusion(f32[2,16,64,64]{3,1,2,0:T(8,128)S(1)} %copy-done.3, f32[2,16,64,64]{3,1,2,0:T(8,128)S(1)} %copy.94, f32[64,1,64,128]{3,2,1,0:T(8,128)S(1)} %get-tuple-element.238, f32[64,1,64,128]{3,2,1,0:T(8,128)S(1)} %get-tuple-element.239, f32[64,1,64,128]{3,2,1,0:T(8,128)S(1)} %get-tuple-element.240), kind=kOutput, calls=%fused_computation.56.clone.1 | convolution fusion | flops 305266688 | bytes 8126464 | tf_op jit(solution)/shard_map/while/body/eval_jaxpr/pbc,bkrc->bkpr/dot_general | solution.py:108
  416.2 3.6 fusion.401
  426.1 14.3 %fusion.403 = f32[64,3,16,64]{3,2,1,0:T(8,128)} fusion(f32[64,1,64,128]{3,2,1,0:T(8,128)S(1)} %copy-done, f32[64,1,64,128]{3,2,1,0:T(8,128)S(1)} %copy-done.1, f32[64,1,64,128]{3,2,1,0:T(8,128)S(1)} %get-tuple-element.233, f32[2,16,64,64]{3,1,2,0:T(8,128)S(1)} %copy.94, f32[2,16,64,64]{3,1,2,0:T(8,128)S(1)} %copy.95), kind=kOutput, calls=%fused_computation.55.clone.1 | convolution fusion | flops 305266688 | bytes 8126464 | tf_op jit(solution)/shard_map/while/body/eval_jaxpr/pbc,bkrc->bkpr/dot_general | solution.py:108
  445.3 13.2 %fusion.406 = f32[64,3,16,64]{3,2,0,1:T(8,128)S(1)} fusion(f32[2,16,64,64]{3,1,2,0:T(8,128)S(1)} %copy-done.3, f32[2,16,64,64]{3,1,2,0:T(8,128)S(1)} %copy.94, f32[64,1,64,128]{3,2,1,0:T(8,128)S(1)} %get-tuple-element.238, f32[64,1,64,128]{3,2,1,0:T(8,128)S(1)} %get-tuple-element.239, f32[64,1,64,128]{3,2,1,0:T(8,128)S(1)} %get-tuple-element.240), kind=kOutput, calls=%fused_computation.56.clone.1 | convolution fusion | flops 305266688 | bytes 8126464 | tf_op jit(solution)/shard_map/while/body/eval_jaxpr/pbc,bkrc->bkpr/dot_general | solution.py:108
  466.7 3.6 fusion.401
  476.6 14.3 %fusion.403 = f32[64,3,16,64]{3,2,1,0:T(8,128)} fusion(f32[64,1,64,128]{3,2,1,0:T(8,128)S(1)} %copy-done, f32[64,1,64,128]{3,2,1,0:T(8,128)S(1)} %copy-done.1, f32[64,1,64,128]{3,2,1,0:T(8,128)S(1)} %get-tuple-element.233, f32[2,16,64,64]{3,1,2,0:T(8,128)S(1)} %copy.94, f32[2,16,64,64]{3,1,2,0:T(8,128)S(1)} %copy.95), kind=kOutput, calls=%fused_computation.55.clone.1 | convolution fusion | flops 305266688 | bytes 8126464 | tf_op jit(solution)/shard_map/while/body/eval_jaxpr/pbc,bkrc->bkpr/dot_general | solution.py:108
  495.8 13.2 %fusion.406 = f32[64,3,16,64]{3,2,0,1:T(8,128)S(1)} fusion(f32[2,16,64,64]{3,1,2,0:T(8,128)S(1)} %copy-done.3, f32[2,16,64,64]{3,1,2,0:T(8,128)S(1)} %copy.94, f32[64,1,64,128]{3,2,1,0:T(8,128)S(1)} %get-tuple-element.238, f32[64,1,64,128]{3,2,1,0:T(8,128)S(1)} %get-tuple-element.239, f32[64,1,64,128]{3,2,1,0:T(8,128)S(1)} %get-tuple-element.240), kind=kOutput, calls=%fused_computation.56.clone.1 | convolution fusion | flops 305266688 | bytes 8126464 | tf_op jit(solution)/shard_map/while/body/eval_jaxpr/pbc,bkrc->bkpr/dot_general | solution.py:108
  517.1 3.6 fusion.401
  527.1 14.3 %fusion.403 = f32[64,3,16,64]{3,2,1,0:T(8,128)} fusion(f32[64,1,64,128]{3,2,1,0:T(8,128)S(1)} %copy-done, f32[64,1,64,128]{3,2,1,0:T(8,128)S(1)} %copy-done.1, f32[64,1,64,128]{3,2,1,0:T(8,128)S(1)} %get-tuple-element.233, f32[2,16,64,64]{3,1,2,0:T(8,128)S(1)} %copy.94, f32[2,16,64,64]{3,1,2,0:T(8,128)S(1)} %copy.95), kind=kOutput, calls=%fused_computation.55.clone.1 | convolution fusion | flops 305266688 | bytes 8126464 | tf_op jit(solution)/shard_map/while/body/eval_jaxpr/pbc,bkrc->bkpr/dot_general | solution.py:108
  546.3 13.2 %fusion.406 = f32[64,3,16,64]{3,2,0,1:T(8,128)S(1)} fusion(f32[2,16,64,64]{3,1,2,0:T(8,128)S(1)} %copy-done.3, f32[2,16,64,64]{3,1,2,0:T(8,128)S(1)} %copy.94, f32[64,1,64,128]{3,2,1,0:T(8,128)S(1)} %get-tuple-element.238, f32[64,1,64,128]{3,2,1,0:T(8,128)S(1)} %get-tuple-element.239, f32[64,1,64,128]{3,2,1,0:T(8,128)S(1)} %get-tuple-element.240), kind=kOutput, calls=%fused_computation.56.clone.1 | convolution fusion | flops 305266688 | bytes 8126464 | tf_op jit(solution)/shard_map/while/body/eval_jaxpr/pbc,bkrc->bkpr/dot_general | solution.py:108
  567.6 3.6 fusion.401
  577.5 14.3 %fusion.403 = f32[64,3,16,64]{3,2,1,0:T(8,128)} fusion(f32[64,1,64,128]{3,2,1,0:T(8,128)S(1)} %copy-done, f32[64,1,64,128]{3,2,1,0:T(8,128)S(1)} %copy-done.1, f32[64,1,64,128]{3,2,1,0:T(8,128)S(1)} %get-tuple-element.233, f32[2,16,64,64]{3,1,2,0:T(8,128)S(1)} %copy.94, f32[2,16,64,64]{3,1,2,0:T(8,128)S(1)} %copy.95), kind=kOutput, calls=%fused_computation.55.clone.1 | convolution fusion | flops 305266688 | bytes 8126464 | tf_op jit(solution)/shard_map/while/body/eval_jaxpr/pbc,bkrc->bkpr/dot_general | solution.py:108
  596.7 13.2 %fusion.406 = f32[64,3,16,64]{3,2,0,1:T(8,128)S(1)} fusion(f32[2,16,64,64]{3,1,2,0:T(8,128)S(1)} %copy-done.3, f32[2,16,64,64]{3,1,2,0:T(8,128)S(1)} %copy.94, f32[64,1,64,128]{3,2,1,0:T(8,128)S(1)} %get-tuple-element.238, f32[64,1,64,128]{3,2,1,0:T(8,128)S(1)} %get-tuple-element.239, f32[64,1,64,128]{3,2,1,0:T(8,128)S(1)} %get-tuple-element.240), kind=kOutput, calls=%fused_computation.56.clone.1 | convolution fusion | flops 305266688 | bytes 8126464 | tf_op jit(solution)/shard_map/while/body/eval_jaxpr/pbc,bkrc->bkpr/dot_general | solution.py:108
  618.0 3.6 fusion.401
  628.0 14.3 %fusion.403 = f32[64,3,16,64]{3,2,1,0:T(8,128)} fusion(f32[64,1,64,128]{3,2,1,0:T(8,128)S(1)} %copy-done, f32[64,1,64,128]{3,2,1,0:T(8,128)S(1)} %copy-done.1, f32[64,1,64,128]{3,2,1,0:T(8,128)S(1)} %get-tuple-element.233, f32[2,16,64,64]{3,1,2,0:T(8,128)S(1)} %copy.94, f32[2,16,64,64]{3,1,2,0:T(8,128)S(1)} %copy.95), kind=kOutput, calls=%fused_computation.55.clone.1 | convolution fusion | flops 305266688 | bytes 8126464 | tf_op jit(solution)/shard_map/while/body/eval_jaxpr/pbc,bkrc->bkpr/dot_general | solution.py:108
  647.2 13.2 %fusion.406 = f32[64,3,16,64]{3,2,0,1:T(8,128)S(1)} fusion(f32[2,16,64,64]{3,1,2,0:T(8,128)S(1)} %copy-done.3, f32[2,16,64,64]{3,1,2,0:T(8,128)S(1)} %copy.94, f32[64,1,64,128]{3,2,1,0:T(8,128)S(1)} %get-tuple-element.238, f32[64,1,64,128]{3,2,1,0:T(8,128)S(1)} %get-tuple-element.239, f32[64,1,64,128]{3,2,1,0:T(8,128)S(1)} %get-tuple-element.240), kind=kOutput, calls=%fused_computation.56.clone.1 | convolution fusion | flops 305266688 | bytes 8126464 | tf_op jit(solution)/shard_map/while/body/eval_jaxpr/pbc,bkrc->bkpr/dot_general | solution.py:108
  678.4 14.3 %fusion.403 = f32[64,3,16,64]{3,2,1,0:T(8,128)} fusion(f32[64,1,64,128]{3,2,1,0:T(8,128)S(1)} %copy-done, f32[64,1,64,128]{3,2,1,0:T(8,128)S(1)} %copy-done.1, f32[64,1,64,128]{3,2,1,0:T(8,128)S(1)} %get-tuple-element.233, f32[2,16,64,64]{3,1,2,0:T(8,128)S(1)} %copy.94, f32[2,16,64,64]{3,1,2,0:T(8,128)S(1)} %copy.95), kind=kOutput, calls=%fused_computation.55.clone.1 | convolution fusion | flops 305266688 | bytes 8126464 | tf_op jit(solution)/shard_map/while/body/eval_jaxpr/pbc,bkrc->bkpr/dot_general | solution.py:108
  697.6 13.2 %fusion.406 = f32[64,3,16,64]{3,2,0,1:T(8,128)S(1)} fusion(f32[2,16,64,64]{3,1,2,0:T(8,128)S(1)} %copy-done.3, f32[2,16,64,64]{3,1,2,0:T(8,128)S(1)} %copy.94, f32[64,1,64,128]{3,2,1,0:T(8,128)S(1)} %get-tuple-element.238, f32[64,1,64,128]{3,2,1,0:T(8,128)S(1)} %get-tuple-element.239, f32[64,1,64,128]{3,2,1,0:T(8,128)S(1)} %get-tuple-element.240), kind=kOutput, calls=%fused_computation.56.clone.1 | convolution fusion | flops 305266688 | bytes 8126464 | tf_op jit(solution)/shard_map/while/body/eval_jaxpr/pbc,bkrc->bkpr/dot_general | solution.py:108
  (441 shorter events, 237.3 us)
Async XLA Ops:
  10.4 3.7 copy-start.8
  18.4 8.0 %copy-start.4 = (f32[64,64,64]{2,0,1:T(8,128)S(1)}, f32[64,64,64]{2,0,1:T(8,128)}, u32[]{:S(2)}) copy-start(f32[64,64,64]{2,0,1:T(8,128)} %fusion.219) | copy-start | bytes 3145732
  38.9 28.7 %all-to-all-start.1 = ((f32[64,1,4096]{2,1,0:T(1,128)}), f32[64,1,4096]{2,1,0:T(1,128)S(1)}, u32[]{:S(2)}, u32[]{:S(2)}) async-start(f32[64,1,4096]{2,1,0:T(1,128)} %reshape.785), calls=%async_computation.1 | async-start | bytes 2097152 | tf_op jit(solution)/shard_map/all_to_all | solution.py:159
  49.8 8.0 %copy-start.5 = (f32[64,64,64]{2,0,1:T(8,128)S(1)}, f32[64,64,64]{2,0,1:T(8,128)}, u32[]{:S(2)}) copy-start(f32[64,64,64]{2,0,1:T(8,128)} %fusion.219) | copy-start | bytes 3145732
  67.6 26.4 %all-to-all-start = ((f32[64,1,4096]{2,1,0:T(1,128)}), f32[64,1,4096]{2,1,0:T(1,128)}, u32[]{:S(2)}, u32[]{:S(2)}) async-start(f32[64,1,4096]{2,1,0:T(1,128)} %reshape.787), calls=%async_computation | async-start | bytes 2097152 | tf_op jit(solution)/shard_map/all_to_all | solution.py:158
  104.0 3.9 copy-start.10
  144.6 6.2 copy-start.6
  163.2 25.8 %all-to-all-start.3 = ((f32[64,1,4096]{2,1,0:T(1,128)}), f32[64,1,4096]{2,1,0:T(1,128)S(1)}, u32[]{:S(2)}, u32[]{:S(2)}) async-start(f32[64,1,4096]{2,1,0:T(1,128)} %reshape.789), calls=%async_computation.3 | async-start | bytes 2097152 | tf_op jit(solution)/shard_map/all_to_all | solution.py:174
  171.3 7.9 %copy-start.7 = (f32[64,64,64]{2,0,1:T(8,128)S(1)}, f32[64,64,64]{2,0,1:T(8,128)}, u32[]{:S(2)}) copy-start(f32[64,64,64]{2,0,1:T(8,128)} %copy-done.6) | copy-start | bytes 3145732
  189.0 26.2 %all-to-all-start.2 = ((f32[64,1,4096]{2,1,0:T(1,128)}), f32[64,1,4096]{2,1,0:T(1,128)}, u32[]{:S(2)}, u32[]{:S(2)}) async-start(f32[64,1,4096]{2,1,0:T(1,128)} %reshape.791), calls=%async_computation.2 | async-start | bytes 2097152 | tf_op jit(solution)/shard_map/all_to_all | solution.py:173
  198.1 84.0 %all-gather.2.cloned.1.call-start = ((), (), s32[]{:S(2)}) async-start(), calls=%async_computation.4 | async-start | bytes 3145728 | tf_op jit(solution)/shard_map/all_gather | solution.py:177
  225.0 4.0 copy-start.9
  243.6 41.6 %copy-start.13 = (f32[2,1,1,8,4096]{4,3,2,1,0:T(8,128)S(1)}, f32[2,1,1,8,4096]{4,3,2,1,0:T(8,128)}, u32[]{:S(2)}) copy-start(f32[2,1,1,8,4096]{4,3,2,1,0:T(8,128)} %param.5) | copy-start | bytes 786436
  283.1 5.4 collective-permute-start
  285.2 6.1 collective-permute-start.1
  312.8 2.5 copy-start.11
  323.0 2.2 copy-start.1
  325.2 14.3 %copy-start.2 = (f32[2,16,64,64]{3,1,2,0:T(8,128)}, f32[2,16,64,64]{3,1,2,0:T(8,128)S(1)}, u32[]{:S(2)}) copy-start(f32[2,16,64,64]{3,1,2,0:T(8,128)S(1)} %copy.95) | copy-start | bytes 1572868 | tf_op jit(solution)/shard_map/while
  342.2 2.2 copy-start.3
  357.6 5.7 copy-start.12
  363.2 2.5 copy-start.11
  375.7 14.3 %copy-start.2 = (f32[2,16,64,64]{3,1,2,0:T(8,128)}, f32[2,16,64,64]{3,1,2,0:T(8,128)S(1)}, u32[]{:S(2)}) copy-start(f32[2,16,64,64]{3,1,2,0:T(8,128)S(1)} %copy.95) | copy-start | bytes 1572868 | tf_op jit(solution)/shard_map/while
  392.6 2.2 copy-start.3
  408.0 5.7 copy-start.12
  413.7 2.5 copy-start.11
  426.1 14.3 %copy-start.2 = (f32[2,16,64,64]{3,1,2,0:T(8,128)}, f32[2,16,64,64]{3,1,2,0:T(8,128)S(1)}, u32[]{:S(2)}) copy-start(f32[2,16,64,64]{3,1,2,0:T(8,128)S(1)} %copy.95) | copy-start | bytes 1572868 | tf_op jit(solution)/shard_map/while
  443.1 2.2 copy-start.3
  458.5 5.7 copy-start.12
  464.2 2.5 copy-start.11
  476.6 14.3 %copy-start.2 = (f32[2,16,64,64]{3,1,2,0:T(8,128)}, f32[2,16,64,64]{3,1,2,0:T(8,128)S(1)}, u32[]{:S(2)}) copy-start(f32[2,16,64,64]{3,1,2,0:T(8,128)S(1)} %copy.95) | copy-start | bytes 1572868 | tf_op jit(solution)/shard_map/while
  493.5 2.2 copy-start.3
  509.0 5.7 copy-start.12
  514.6 2.5 copy-start.11
  527.0 14.3 %copy-start.2 = (f32[2,16,64,64]{3,1,2,0:T(8,128)}, f32[2,16,64,64]{3,1,2,0:T(8,128)S(1)}, u32[]{:S(2)}) copy-start(f32[2,16,64,64]{3,1,2,0:T(8,128)S(1)} %copy.95) | copy-start | bytes 1572868 | tf_op jit(solution)/shard_map/while
  544.0 2.2 copy-start.3
  559.4 5.7 copy-start.12
  565.1 2.5 copy-start.11
  577.5 14.3 %copy-start.2 = (f32[2,16,64,64]{3,1,2,0:T(8,128)}, f32[2,16,64,64]{3,1,2,0:T(8,128)S(1)}, u32[]{:S(2)}) copy-start(f32[2,16,64,64]{3,1,2,0:T(8,128)S(1)} %copy.95) | copy-start | bytes 1572868 | tf_op jit(solution)/shard_map/while
  594.5 2.2 copy-start.3
  609.9 5.7 copy-start.12
  615.5 2.5 copy-start.11
  628.0 14.3 %copy-start.2 = (f32[2,16,64,64]{3,1,2,0:T(8,128)}, f32[2,16,64,64]{3,1,2,0:T(8,128)S(1)}, u32[]{:S(2)}) copy-start(f32[2,16,64,64]{3,1,2,0:T(8,128)S(1)} %copy.95) | copy-start | bytes 1572868 | tf_op jit(solution)/shard_map/while
  644.9 2.2 copy-start.3
  660.3 5.7 copy-start.12
  666.0 2.5 copy-start.11
  678.4 14.3 %copy-start.2 = (f32[2,16,64,64]{3,1,2,0:T(8,128)}, f32[2,16,64,64]{3,1,2,0:T(8,128)S(1)}, u32[]{:S(2)}) copy-start(f32[2,16,64,64]{3,1,2,0:T(8,128)S(1)} %copy.95) | copy-start | bytes 1572868 | tf_op jit(solution)/shard_map/while
  695.4 2.2 copy-start.3
  710.8 5.7 copy-start.12
  (15 other events, 28.3 us)
Sparse Core Ops, SparseCore 0:
  245.4 36.6 all-gather.1
where the time goes:
time: 737 us; the launch traced here: 724 us
  matrix products  355 us (48%)
  local copies, waits for them, and re-layouts  135 us (18%)
  other arithmetic  96 us (13%)
  waiting for transfers between devices  44.9 us (6%)
  starting transfers between devices  40.1 us (5%)
  loops' own time  38 us (5%)
  between operations  14.8 us (2%)
    dot_general x16, matrix products, lens_fields(): jnp.einsum('pbc,bkrc->bkpr', plane_blocks, x_weights, precision=lax.Preci...  220 us
    dot_general x14, matrix products, contract_second(): jnp.einsum('...kb,bm->...mk', values, table, precision=lax.Precision.HIGH...  93.6 us
    select_n x16, other arithmetic, spline_terms(): jnp.where(inside, 2.0 / 3.0 - magnitude * magnitude + 0.5 * magnitude * m...  46.9 us
    dot_general x14, matrix products, contract_first(): jnp.einsum('...ab,ak->...kb', values, table, precision=lax.Precision.HIGH...  41.6 us
    another operation x1, loops' own time, on_device(): deflect, jacob = lax.map(one_row, jnp.arange(ray_count, dtype=jnp.int32))  38 us
    all_gather x1, waiting for transfers between devices, on_device(): together = lax.all_gather(potential[None], 'plane', axis=0, tiled=True)  36.8 us
    dynamic_update_slice x32, local copies, waits for them, and re-layouts, on_device(): deflect, jacob = lax.map(one_row, jnp.arange(ray_count, dtype=jnp.int32))  30.1 us
    reduce_sum x16, other arithmetic, lens_fields(): bend_down = jnp.sum(down_curves * across[:, 0], axis=1)  29.4 us
  transfers between devices with their start and end apart: 7, of which 5 were waited for; matrix products, arithmetic and copies ran while one was open for 9% of the time, Pallas kernels for 0%

commit v1 on v0

v1 whole, which is shorter than its diff:
```python
import functools
import math

import jax
import jax.numpy as jnp
import numpy as np
from jax import lax
from jax.experimental import pallas as pl
from jax.experimental.pallas import tpu as pltpu
from jax.sharding import PartitionSpec as P

N = 4096
OUTER = 32
SLABS = 64
WIN = 48
LEAD = 5
HIGHEST = lax.Precision.HIGHEST
lens_ratio = 0.5
screen_modes = 4.0


def angles(left, right, length):
    return (np.outer(left, right) % length) * (2.0 * np.pi / length)


def cas_pair(left, right, length):
    a = angles(left, right, length)
    return np.cos(a) + np.sin(a), np.cos(a) - np.sin(a)


def f32(table):
    return np.asarray(table, np.float32)


@functools.cache
def tables():
    out = {}
    lane = np.arange(128)
    plus, minus = cas_pair(lane, lane, 128)
    out["row_fwd"] = f32(np.concatenate([plus.T, minus.T], axis=1))
    turn = angles(np.arange(OUTER), lane, N)
    out["row_turn"] = f32(np.stack([np.cos(turn), np.sin(turn)]))
    out["row_inv"] = f32(0.5 * np.concatenate([plus, -minus], axis=1))
    sixty = np.arange(64)
    plus, minus = cas_pair(sixty, sixty, 64)
    two = np.eye(2)
    out["col_fwd"] = f32(np.concatenate([np.kron(two, plus), np.kron(two, minus)], axis=0))
    turn = angles(sixty, np.concatenate([sixty, sixty]), N)
    out["col_turn"] = f32(np.stack([np.cos(turn), np.sin(turn)]))
    inv, turns = [], []
    for p in range(2):
        rows = 32 * p - LEAD + np.arange(WIN)
        plus, minus = cas_pair(sixty, rows, 64)
        pad = np.zeros((128, 32))
        inv.append(np.concatenate([np.kron(two, plus), pad, -np.kron(two, minus), pad], axis=1))
        turn = angles(sixty, np.concatenate([rows, rows, np.zeros(32, rows.dtype)]), N)
        turns.append(np.stack([np.cos(turn), np.sin(turn)]))
    out["col_inv"] = f32(0.5 * np.stack(inv))
    out["col_back"] = f32(np.stack(turns))
    ids = np.arange(64)[:, None] + 64 * np.concatenate([sixty, sixty])[None, :]
    wave = 2.0 * np.pi / N * np.minimum(ids, N - ids)
    out["wave2"] = f32(wave**2)
    return out


def cmul(re, im, c, s):
    if abs(s) < 1e-12 and abs(c - 1.0) < 1e-12:
        return re, im
    if abs(c) < 1e-12 and abs(s - 1.0) < 1e-12:
        return (None if im is None else -im), re
    if im is None:
        return re * c, re * s
    if re is None:
        return im * (-s), im * c
    if abs(c - s) < 1e-12:
        return (re - im) * c, (re + im) * c
    if abs(c + s) < 1e-12:
        return (re + im) * c, (im - re) * c
    return re * c - im * s, re * s + im * c


def add(a, b):
    return b if a is None else a if b is None else a + b


def sub(a, b):
    return a if b is None else -b if a is None else a - b


def neg(a):
    return None if a is None else -a


def real_to_half(xs):
    n = len(xs)
    if n == 2:
        return [(xs[0] + xs[1], None), (xs[0] - xs[1], None)]
    even, odd = real_to_half(xs[0::2]), real_to_half(xs[1::2])
    half = n // 2
    out = [None] * (half + 1)
    for k in range(half // 2 + 1):
        c, s = math.cos(2 * math.pi * k / n), math.sin(2 * math.pi * k / n)
        tr, ti = cmul(*odd[k], c, s)
        er, ei = even[k]
        out[k] = (add(er, tr), add(ei, ti))
        if half - k != k:
            out[half - k] = (sub(er, tr), sub(ti, ei))
    return out


def half_to_real(xs):
    half = len(xs) - 1
    n = 2 * half
    if n == 2:
        return [xs[0][0] + xs[1][0], xs[0][0] - xs[1][0]]
    even, odd = [], []
    for k in range(half // 2 + 1):
        ar, ai = xs[k]
        br, bi = xs[half - k]
        if k == half - k:
            even.append((ar + ar, None))
            odd.append((-(ai + ai), None))
            continue
        even.append((add(ar, br), sub(ai, bi)))
        c, s = math.cos(2 * math.pi * k / n), math.sin(2 * math.pi * k / n)
        odd.append(cmul(sub(ar, br), add(ai, bi), c, s))
    evens, odds = half_to_real(even), half_to_real(odd)
    return [v for pair in zip(evens, odds) for v in pair]


def row8(ref, *index):
    return jnp.broadcast_to(ref[index], (8, 128))


def turned(re, im, c, s):
    if im is None:
        return re * c, re * s
    return re * c - im * s, re * s + im * c


def forward_outer(xs, turn_ref, store):
    n = len(xs)
    half = real_to_half(xs)
    for m in range(n):
        re, im = half[m] if m <= n // 2 else (half[n - m][0], neg(half[n - m][1]))
        store(m, *turned(re, im, row8(turn_ref, 0, slice(m, m + 1)), row8(turn_ref, 1, slice(m, m + 1))))


def inverse_outer(load, n, turn_ref, *lead):
    def value(m):
        re, im = load(m)
        return turned(re, im, row8(turn_ref, *lead, 0, slice(m, m + 1)), row8(turn_ref, *lead, 1, slice(m, m + 1)))

    spectrum = []
    for m in range(n // 2 + 1):
        re, im = value(m)
        if m in (0, n // 2):
            spectrum.append((re + re, None))
        else:
            ro, io = value(n - m)
            spectrum.append((re + ro, im - io))
    return half_to_real(spectrum)


def rows_kernel(kappa_ref, weight_ref, turn_ref, out_ref, mid):
    def group(g, carry):
        rows = pl.ds(pl.multiple_of(8 * g, 8), 8)
        xs = [kappa_ref[rows, 128 * j : 128 * j + 128] for j in range(OUTER)]

        def store(m, re, im):
            spot = pl.ds(pl.multiple_of(64 * m + 8 * g, 8), 8)
            mid[spot, 0:128] = re
            mid[spot, 128:256] = im

        forward_outer(xs, turn_ref, store)
        return carry

    lax.fori_loop(0, 8, group, 0)

    def pair(i, carry):
        spot = pl.ds(pl.multiple_of(128 * i, 128), 128)
        out_ref[spot, :] = lax.dot_general(
            weight_ref[...], mid[spot, :], (((1,), (1,)), ((), ())),
            precision=HIGHEST, preferred_element_type=jnp.float32,
        )
        return carry

    lax.fori_loop(0, 16, pair, 0)


def columns_kernel(in_ref, fwd_ref, turn_ref, wave_ref, inv_ref, back_ref, out_ref, mid, spec, strips):
    owner = lax.axis_index("slab")
    base = 2 * lax.div(owner, 4) + 1024 * lax.rem(owner, 4)
    lane = lax.broadcasted_iota(jnp.int32, (8, 128), 1)
    sub8 = lax.broadcasted_iota(jnp.int32, (8, 128), 0)
    screen = (2.0 * math.pi * screen_modes / N) ** 2

    def group(g, carry):
        rows = pl.ds(pl.multiple_of(8 * g, 8), 8)
        xs = [in_ref[s, rows, :] for s in range(SLABS)]

        def store(m, re, im):
            mid[8 * m : 8 * m + 8, 0:128] = re
            mid[8 * m : 8 * m + 8, 128:256] = im

        forward_outer(xs, turn_ref, store)
        spec[...] = jnp.dot(mid[...], fwd_ref[...], precision=HIGHEST, preferred_element_type=jnp.float32)
        ids = base + jnp.where(lane >= 64, 1, 0) + 32 * (8 * g + sub8)
        wave = (2.0 * math.pi / N) * jnp.minimum(ids, N - ids).astype(jnp.float32)
        mine = wave * wave + screen
        for m in range(SLABS):
            factor = -2.0 / ((mine + row8(wave_ref, slice(m, m + 1))) * float(N * N))
            if m == 0:
                factor = jnp.where((ids == 0) & (lane == 0), 0.0, factor)
            spec[8 * m : 8 * m + 8, :] = spec[8 * m : 8 * m + 8, :] * factor
        for p in range(2):
            mid[...] = jnp.dot(spec[...], inv_ref[p], precision=HIGHEST, preferred_element_type=jnp.float32)
            values = inverse_outer(
                lambda m: (mid[8 * m : 8 * m + 8, 0:128], mid[8 * m : 8 * m + 8, 128:256]), SLABS, back_ref, p
            )
            for s in range(SLABS):
                strips[p * SLABS + s, rows, :] = values[s]
        return carry

    lax.fori_loop(0, 4, group, 0)

    def pack(d, carry):
        last = strips[d, 24:32, :]
        for k in range(3):
            moved = last if k == 3 else pltpu.roll(last, (96 - 32 * k) % 128, 1)
            out_ref[d, 8 * k : 8 * k + 8, :] = jnp.where(lane < 96, strips[d, 8 * k : 8 * k + 8, :], moved)
        return carry

    lax.fori_loop(0, 2 * SLABS, pack, 0, unroll=4)


def spline_weights(f):
    e = 1.0 - f
    f2, e2 = f * f, e * e
    f3, e3 = f2 * f, e2 * e
    sixth, third = 1.0 / 6.0, 2.0 / 3.0
    value = [e3 * sixth, third - f2 + 0.5 * f3, third - e2 + 0.5 * e3, f3 * sixth]
    slope = [-0.5 * e2, 1.5 * f2 - 2.0 * f, 2.0 * e - 1.5 * e2, 0.5 * f2]
    curve = [e, 3.0 * f - 2.0, 1.0 - 3.0 * f, f]
    return value, slope, curve


def dot4(ws, vs):
    return (ws[0] * vs[0] + ws[1] * vs[1]) + (ws[2] * vs[2] + ws[3] * vs[3])


def stencil(taps, xw, yw):
    flat = [dot4(xw[0], row) for row in taps]
    slope = [dot4(xw[1], row) for row in taps]
    curve = [dot4(xw[2], row) for row in taps]
    return dot4(yw[1], flat), dot4(yw[0], slope), dot4(yw[2], flat), dot4(yw[0], curve), dot4(yw[1], slope)


def rays_kernel(in_ref, inv_ref, turn_ref, off_ref, deflect_ref, jacob_ref, mid, near, even, odd):
    lane = lax.broadcasted_iota(jnp.int32, (8, 128), 1)

    for q in range(2):
        def unpack(i, carry):
            parts = []
            for d in range(4):
                got = [in_ref[q * SLABS + 4 * i + d, 8 * k : 8 * k + 8, :] for k in range(3)]
                moved = [pltpu.roll(got[k], 32 + 32 * k, 1) for k in range(3)]
                parts += got
                parts.append(jnp.where(lane < 32, moved[0], jnp.where(lane < 64, moved[1], moved[2])))
            block = jnp.transpose(jnp.concatenate(parts, axis=0))[: 2 * WIN]
            spot = pl.ds(pl.multiple_of(2 * WIN * i, 8), 2 * WIN)
            mid[spot, :] = jnp.dot(block, inv_ref[...], precision=HIGHEST, preferred_element_type=jnp.float32)
            return carry

        lax.fori_loop(0, 16, unpack, 0)

        def finish(g, carry):
            def load(m):
                spot = pl.ds(pl.multiple_of(WIN * m + 8 * g, 8), 8)
                return mid[spot, 0:128], mid[spot, 128:256]

            values = inverse_outer(load, OUTER, turn_ref)

            def spot(t):
                return pl.ds(pl.multiple_of(WIN * t + 8 * g, 8), 8)

            if q == 0:
                for t in range(OUTER):
                    near[2, spot(t), :] = values[t]
                for d in (-2, -1, 1, 2):
                    moved = [pltpu.roll(v, (-d) % 128, 1) for v in values]
                    for t in range(OUTER):
                        if d < 0:
                            v = jnp.where(lane < -d, moved[t - 1], moved[t])
                        else:
                            v = jnp.where(lane < 128 - d, moved[t], moved[(t + 1) % OUTER])
                        near[2 + d, spot(t), :] = v
            else:
                moved = [pltpu.roll(v, 32, 1) for v in values]
                for t in range(OUTER):
                    even[spot(t), :] = jnp.where(lane < 32, moved[t - 1], moved[t])
                moved = [pltpu.roll(v, 96, 1) for v in values]
                for t in range(OUTER):
                    odd[spot(t), :] = jnp.where(lane < 96, moved[t], moved[(t + 1) % OUTER])
            return carry

        lax.fori_loop(0, WIN // 8, finish, 0)

    def tile(t, carry):
        cols = pl.ds(pl.multiple_of(128 * t, 128), 128)
        off_y = off_ref[0, :, cols]
        off_x = off_ref[1, :, cols]
        zero = jnp.zeros((8, 128), jnp.float32)
        rel_y = 4.0 * off_y
        low_y = jnp.floor(rel_y)
        left = off_x < 0.0
        frac_x = jnp.where(left, off_x + 1.0, off_x)
        hit = {v: low_y == float(v) for v in range(-2, 3)}
        taps = [[zero] * 4 for _ in range(4)]
        for j in range(4, 11):
            rows = [near[d, pl.ds(WIN * t + j, 8, stride=4), :] for d in range(5)]
            cells = [jnp.where(left, rows[c], rows[c + 1]) for c in range(4)]
            for r in range(4):
                if j - 6 - r in hit:
                    for c in range(4):
                        taps[r][c] = jnp.where(hit[j - 6 - r], cells[c], taps[r][c])
        first = stencil(taps, spline_weights(frac_x), spline_weights(rel_y - low_y))
        pos_y = (7.0 + rel_y) - lens_ratio * first[0]
        start = (32 + lax.rem(lane, 64)).astype(jnp.float32)
        pos_x = (start + off_x) - lens_ratio * first[1]
        low_y = jnp.floor(pos_y)
        low_x = jnp.floor(pos_x)
        xw = spline_weights(pos_x - low_x)
        yw = spline_weights(pos_y - low_y)
        cell_x = jnp.clip(low_x, -8.0, 136.0).astype(jnp.int32)
        cell_y = jnp.clip(low_y, -8.0, 32.0).astype(jnp.int32)
        spots = [cell_x + (c - 1) for c in range(4)]
        inside = [(s >= 0) & (s < 128) for s in spots]
        xw = [[jnp.where(inside[c], w[c], 0.0) for c in range(4)] for w in xw]
        spots = [jnp.clip(s, 0, 127) for s in spots]
        is_even = lane < 64
        hit = {v: cell_y == v for v in range(-2, 17)}
        taps = [[zero] * 4 for _ in range(4)]
        for j in range(16):
            ev = even[pl.ds(WIN * t + j, 8, stride=4), :]
            od = odd[pl.ds(WIN * t + j, 8, stride=4), :]
            for c in range(4):
                cell = jnp.where(
                    is_even,
                    jnp.take_along_axis(ev, spots[c], axis=1),
                    jnp.take_along_axis(od, spots[c], axis=1),
                )
                for r in range(4):
                    taps[r][c] = jnp.where(hit[j + 1 - r], cell, taps[r][c])
        second = stencil(taps, xw, yw)
        hess_yy, hess_xx, hess_xy = first[2], first[3], first[4]
        other_yy, other_xx, other_xy = second[2], second[3], second[4]
        lensed_yy = 1.0 - lens_ratio * hess_yy
        lensed_xx = 1.0 - lens_ratio * hess_xx
        lensed_xy = -lens_ratio * hess_xy
        deflect_ref[0, :, cols] = first[0] + second[0]
        deflect_ref[1, :, cols] = first[1] + second[1]
        jacob_ref[0, :, cols] = 1.0 - hess_yy - (other_yy * lensed_yy + other_xy * lensed_xy)
        jacob_ref[1, :, cols] = -hess_xy - (other_yy * lensed_xy + other_xy * lensed_xx)
        jacob_ref[2, :, cols] = -hess_xy - (other_xy * lensed_yy + other_xx * lensed_xy)
        jacob_ref[3, :, cols] = 1.0 - hess_xx - (other_xy * lensed_xy + other_xx * lensed_xx)
        return carry

    lax.fori_loop(0, OUTER, tile, 0)


def vmem(shape):
    return pltpu.VMEM(shape, jnp.float32)


def call(kernel, name, args, outs, scratch):
    return pl.pallas_call(
        kernel,
        name=name,
        out_shape=outs,
        in_specs=[pl.BlockSpec(memory_space=pltpu.VMEM)] * len(args),
        out_specs=jax.tree.map(lambda _: pl.BlockSpec(memory_space=pltpu.VMEM), outs),
        scratch_shapes=scratch,
        compiler_params=pltpu.CompilerParams(vmem_limit_bytes=60 * 1024 * 1024),
    )(*args)


def shape(*dims):
    return jax.ShapeDtypeStruct(dims, jnp.float32)


def on_device(kappa, ray_offsets):
    tab = tables()
    spectra = call(
        rows_kernel, "rows", (kappa[0], tab["row_fwd"], tab["row_turn"]), shape(2048, 128), [vmem((2048, 256))]
    )
    columns = lax.all_to_all(spectra.reshape(SLABS, 32, 128), "slab", split_axis=0, concat_axis=0, tiled=True)
    strips = call(
        columns_kernel,
        "columns",
        (columns, tab["col_fwd"], tab["col_turn"], tab["wave2"], tab["col_inv"], tab["col_back"]),
        shape(2 * SLABS, 24, 128),
        [vmem((512, 256)), vmem((512, 128)), vmem((2 * SLABS, 32, 128))],
    )
    windows = lax.all_to_all(strips, ("plane", "slab"), split_axis=0, concat_axis=0, tiled=True)
    deflection, jacobian = call(
        rays_kernel,
        "rays",
        (windows, tab["row_inv"], tab["row_turn"], ray_offsets[:, 0, 0]),
        (shape(2, 8, N), shape(4, 8, N)),
        [vmem((OUTER * WIN, 256)), vmem((5, OUTER * WIN, 128)), vmem((OUTER * WIN, 128)), vmem((OUTER * WIN, 128))],
    )
    return deflection[:, None, None], jacobian[:, None, None]


def solution(mesh):
    placed = (P("plane", "slab", None), P(None, "slab", "plane", None, None))
    return jax.shard_map(
        on_device,
        mesh=mesh,
        in_specs=placed,
        out_specs=(P(None, "slab", "plane", None, None), P(None, "slab", "plane", None, None)),
        check_vma=False,
    )
```

time: 737 us -> 112 us (0.15); the launches traced: 724 us -> 112 us
  matrix products: 355 us -> 0 us
  local copies, waits for them, and re-layouts: 135 us -> 0 us
  other arithmetic: 96 us -> 0 us
  blocking collectives: 0 us -> 59 us
  Pallas kernels: 0 us -> 52.5 us
  waiting for transfers between devices: 44.9 us -> 0 us
  starting transfers between devices: 40.1 us -> 0 us
  loops' own time: 38 us -> 0 us
  between operations: 14.8 us -> 0.63 us
    dot_general x44 -> x0, matrix products: 355 us -> none  [the longest x16 220 us: lens_fields(): jnp.einsum('pbc,bkrc->bkpr', plane_blocks, x_weights, precision=lax.Preci...]
    all_to_all x0 -> x2, blocking collectives: none -> 59 us  [the longest x1 30.8 us: on_device(): lax.all_to_all(strips, ('plane', 'slab'), split_axis=0, concat_axis=0, ti...]
    pallas_call x0 -> x3, Pallas kernels: none -> 52.5 us  [call(): pl.pallas_call(kernel, name=name, out_shape=outs, in_specs=[pl.BlockSpec(...]
    select_n x16 -> x0, other arithmetic: 46.9 us -> none  [spline_terms(): jnp.where(inside, 2.0 / 3.0 - magnitude * magnitude + 0.5 * magnitude * m...]
    another operation x1 -> x0, loops' own time: 38 us -> none  [on_device(): deflect, jacob = lax.map(one_row, jnp.arange(ray_count, dtype=jnp.int32))]
    all_to_all x4 -> x0, starting transfers between devices: 37.6 us -> none  [the longest x1 10.9 us: on_device(): lax.all_to_all(row_imag, 'slab', split_axis=1, concat_axis=1, tiled=True)]
    all_gather x1 -> x0, waiting for transfers between devices: 36.8 us -> none  [on_device(): together = lax.all_gather(potential[None], 'plane', axis=0, tiled=True)]
    dynamic_update_slice x32 -> x0, local copies, waits for them, and re-layouts: 30.1 us -> none  [on_device(): deflect, jacob = lax.map(one_row, jnp.arange(ray_count, dtype=jnp.int32))]
  transfers between devices with their start and end apart: 7 -> 0, of which waited for: 5 -> 0; matrix products, arithmetic and copies ran while one was open for 9% -> 0% of each run, Pallas kernels for 0% -> 0%
where the time goes in v1:
time: 112 us
  blocking collectives  59 us (53%)
  Pallas kernels  52.5 us (47%)
    pallas_call x3, Pallas kernels, call(): pl.pallas_call(kernel, name=name, out_shape=outs, in_specs=[pl.BlockSpec(...  52.5 us
    all_to_all x1, blocking collectives, on_device(): lax.all_to_all(strips, ('plane', 'slab'), split_axis=0, concat_axis=0, ti...  30.8 us
    all_to_all x1, blocking collectives, on_device(): lax.all_to_all(spectra.reshape(SLABS, 32, 128), 'slab', split_axis=0, con...  28.2 us

profile of v1, /device:TPU:1, one launch (start us, length us, event | category | flops | bytes accessed | tf_op | source)
XLA Modules:
  0.0 112.1 jit_solution(7847473562494841145)
XLA Ops:
  0.6 7.3 %rows.1 = f32[2048,128]{1,0:T(8,128)} custom-call(f32[64,4096]{1,0:T(8,128)} %bitcast.10, f32[128,256]{1,0:T(8,128)} %constant.16.clone.weight_ref, f32[2,32,128]{2,1,0:T(8,128)} %constant.17.clone.turn_ref), custom_call_target="tpu_custom_call" | custom-call | tf_op jit(solution)/shard_map/rows/pallas_call | solution.py:377
  7.9 28.2 %all_to_all.10.in_ref = f32[64,32,128]{2,1,0:T(8,128)} all-to-all(f32[64,32,128]{2,1,0:T(8,128)} %bitcast.9), channel_id=1, replica_groups=mesh['plane'=2,'slab'=64] {'slab'}, dimensions={0} | all-to-all | bytes 2097152 | tf_op jit(solution)/shard_map/all_to_all | solution.py:397
  36.2 14.8 %columns.1 = f32[128,24,128]{2,1,0:T(8,128)} custom-call(f32[64,32,128]{2,1,0:T(8,128)} %all_to_all.10.in_ref, f32[256,128]{1,0:T(8,128)} %constant.18.clone.fwd_ref, f32[2,64,128]{2,1,0:T(8,128)} %constant.19.clone.turn_ref, f32[64,128]{1,0:T(8,128)} %constant.20.clone.wave_ref, f32[2,128,256]{2,1,0:T(8,128)} %constant.21.clone.inv_ref, ...), custom_call_target="tpu_custom_call" | custom-call | tf_op jit(solution)/shard_map/columns/pallas_call | solution.py:377
  51.0 30.8 %all_to_all.11.in_ref = f32[128,24,128]{2,1,0:T(8,128)} all-to-all(f32[128,24,128]{2,1,0:T(8,128)} %columns.1), channel_id=1, replica_groups=mesh['plane'=2,'slab'=64] {'plane','slab'}, dimensions={0} | all-to-all | bytes 3145728 | tf_op jit(solution)/shard_map/all_to_all | solution.py:405
  81.8 30.4 %rays.1 = (f32[2,8,4096]{2,1,0:T(8,128)}, f32[4,8,4096]{2,1,0:T(8,128)}) custom-call(f32[128,24,128]{2,1,0:T(8,128)} %all_to_all.11.in_ref, f32[128,256]{1,0:T(8,128)} %constant.23.clone.inv_ref, f32[2,32,128]{2,1,0:T(8,128)} %constant.17.clone.turn_ref, f32[2,8,4096]{2,1,0:T(8,128)} %bitcast.11), custom_call_target="tpu_custom_call" | custom-call | tf_op jit(solution)/shard_map/rays/pallas_call | solution.py:377

commit v2 on v1

--- a/solution.py
+++ b/solution.py
@@ -12,9 +12,10 @@
 N = 4096
 OUTER = 32
 SLABS = 64
+PATCH_ROWS = 16
 WIN = 48
+UNROLL = 1
 LEAD = 5
-HIGHEST = lax.Precision.HIGHEST
 lens_ratio = 0.5
 screen_modes = 4.0
 
@@ -30,6 +31,14 @@
 
 def f32(table):
     return np.asarray(table, np.float32)
+
+
+def parts(table, count):
+    out = []
+    for _ in range(count):
+        out.append(np.asarray(table, jnp.bfloat16))
+        table = table - np.asarray(out[-1], np.float64)
+    return out
 
 
 @functools.cache
@@ -37,14 +46,15 @@
     out = {}
     lane = np.arange(128)
     plus, minus = cas_pair(lane, lane, 128)
-    out["row_fwd"] = f32(np.concatenate([plus.T, minus.T], axis=1))
+    out["row_fwd"] = np.concatenate(parts(np.concatenate([plus.T, minus.T], axis=1), 2), axis=0)
     turn = angles(np.arange(OUTER), lane, N)
     out["row_turn"] = f32(np.stack([np.cos(turn), np.sin(turn)]))
-    out["row_inv"] = f32(0.5 * np.concatenate([plus, -minus], axis=1))
+    out["row_inv"] = np.stack(parts(0.5 * np.concatenate([plus, -minus], axis=1), 3))
     sixty = np.arange(64)
     plus, minus = cas_pair(sixty, sixty, 64)
     two = np.eye(2)
-    out["col_fwd"] = f32(np.concatenate([np.kron(two, plus), np.kron(two, minus)], axis=0))
+    both = np.concatenate([np.kron(two, plus), np.kron(two, minus)], axis=0)
+    out["col_fwd"] = np.concatenate(parts(both, 2), axis=1)
     turn = angles(sixty, np.concatenate([sixty, sixty]), N)
     out["col_turn"] = f32(np.stack([np.cos(turn), np.sin(turn)]))
     inv, turns = [], []
@@ -55,7 +65,7 @@
         inv.append(np.concatenate([np.kron(two, plus), pad, -np.kron(two, minus), pad], axis=1))
         turn = angles(sixty, np.concatenate([rows, rows, np.zeros(32, rows.dtype)]), N)
         turns.append(np.stack([np.cos(turn), np.sin(turn)]))
-    out["col_inv"] = f32(0.5 * np.stack(inv))
+    out["col_inv"] = np.stack([np.stack(parts(0.5 * table, 3)) for table in inv])
     out["col_back"] = f32(np.stack(turns))
     ids = np.arange(64)[:, None] + 64 * np.concatenate([sixty, sixty])[None, :]
     wave = 2.0 * np.pi / N * np.minimum(ids, N - ids)
@@ -162,6 +172,23 @@
     return half_to_real(spectrum)
 
 
+def split(x, count):
+    out = []
+    for i in range(count):
+        out.append(x.astype(jnp.bfloat16))
+        if i + 1 < count:
+            x = x - out[-1].astype(jnp.float32)
+    return out
+
+
+def fine_dot(x, w):
+    a, b, c = split(x, 3)
+    w0, w1, w2 = w[0], w[1], w[2]
+    left = jnp.concatenate([a, b, a, b, a, c], axis=1)
+    right = jnp.concatenate([w0, w0, w1, w1, w2, w0], axis=0)
+    return jnp.dot(left, right, preferred_element_type=jnp.float32)
+
+
 def rows_kernel(kappa_ref, weight_ref, turn_ref, out_ref, mid):
     def group(g, carry):
         rows = pl.ds(pl.multiple_of(8 * g, 8), 8)
@@ -179,10 +206,10 @@
 
     def pair(i, carry):
         spot = pl.ds(pl.multiple_of(128 * i, 128), 128)
-        out_ref[spot, :] = lax.dot_general(
-            weight_ref[...], mid[spot, :], (((1,), (1,)), ((), ())),
-            precision=HIGHEST, preferred_element_type=jnp.float32,
-        )
+        left = jnp.concatenate([weight_ref[...]] * 2, axis=1)
+        right = jnp.concatenate(split(mid[spot, :], 2), axis=1)
+        both = lax.dot_general(left, right, (((1,), (1,)), ((), ())), preferred_element_type=jnp.float32)
+        out_ref[spot, :] = both[:128] + both[128:]
         return carry
 
     lax.fori_loop(0, 16, pair, 0)
@@ -204,7 +231,10 @@
             mid[8 * m : 8 * m + 8, 128:256] = im
 
         forward_outer(xs, turn_ref, store)
-        spec[...] = jnp.dot(mid[...], fwd_ref[...], precision=HIGHEST, preferred_element_type=jnp.float32)
+        left = jnp.concatenate(split(mid[...], 2), axis=1)
+        right = jnp.concatenate([fwd_ref[...]] * 2, axis=0)
+        both = jnp.dot(left, right, preferred_element_type=jnp.float32)
+        spec[...] = both[:, :128] + both[:, 128:]
         ids = base + jnp.where(lane >= 64, 1, 0) + 32 * (8 * g + sub8)
         wave = (2.0 * math.pi / N) * jnp.minimum(ids, N - ids).astype(jnp.float32)
         mine = wave * wave + screen
@@ -214,7 +244,7 @@
                 factor = jnp.where((ids == 0) & (lane == 0), 0.0, factor)
             spec[8 * m : 8 * m + 8, :] = spec[8 * m : 8 * m + 8, :] * factor
         for p in range(2):
-            mid[...] = jnp.dot(spec[...], inv_ref[p], precision=HIGHEST, preferred_element_type=jnp.float32)
+            mid[...] = fine_dot(spec[...], inv_ref[p])
             values = inverse_outer(
                 lambda m: (mid[8 * m : 8 * m + 8, 0:128], mid[8 * m : 8 * m + 8, 128:256]), SLABS, back_ref, p
             )
@@ -250,10 +280,26 @@
 
 
 def stencil(taps, xw, yw):
-    flat = [dot4(xw[0], row) for row in taps]
-    slope = [dot4(xw[1], row) for row in taps]
-    curve = [dot4(xw[2], row) for row in taps]
+    rows = list(zip(*taps))
+    flat = [dot4(xw[0], row) for row in rows]
+    slope = [dot4(xw[1], row) for row in rows]
+    curve = [dot4(xw[2], row) for row in rows]
     return dot4(yw[1], flat), dot4(yw[0], slope), dot4(yw[2], flat), dot4(yw[0], curve), dot4(yw[1], slope)
+
+
+def kept(weights, first, count):
+    inside = [(first + c >= 0) & (first + c < count) for c in range(4)]
+    return [[jnp.where(inside[c], w[c], 0.0) for c in range(4)] for w in weights]
+
+
+def lane_gather(values, spots):
+    dims = lax.GatherDimensionNumbers(
+        offset_dims=(), collapsed_slice_dims=(1,), start_index_map=(1,),
+        operand_batching_dims=(0,), start_indices_batching_dims=(0,),
+    )
+    return lax.gather(
+        values, spots[..., None], dims, (1, 1), mode=lax.GatherScatterMode.PROMISE_IN_BOUNDS
+    )
 
 
 def rays_kernel(in_ref, inv_ref, turn_ref, off_ref, deflect_ref, jacob_ref, mid, near, even, odd):
@@ -269,7 +315,7 @@
                 parts.append(jnp.where(lane < 32, moved[0], jnp.where(lane < 64, moved[1], moved[2])))
             block = jnp.transpose(jnp.concatenate(parts, axis=0))[: 2 * WIN]
             spot = pl.ds(pl.multiple_of(2 * WIN * i, 8), 2 * WIN)
-            mid[spot, :] = jnp.dot(block, inv_ref[...], precision=HIGHEST, preferred_element_type=jnp.float32)
+            mid[spot, :] = fine_dot(block, inv_ref[...])
             return carry
 
         lax.fori_loop(0, 16, unpack, 0)
@@ -310,48 +356,44 @@
         cols = pl.ds(pl.multiple_of(128 * t, 128), 128)
         off_y = off_ref[0, :, cols]
         off_x = off_ref[1, :, cols]
-        zero = jnp.zeros((8, 128), jnp.float32)
         rel_y = 4.0 * off_y
-        low_y = jnp.floor(rel_y)
+        low_y = jnp.minimum(jnp.floor(rel_y), 1.0)
         left = off_x < 0.0
         frac_x = jnp.where(left, off_x + 1.0, off_x)
-        hit = {v: low_y == float(v) for v in range(-2, 3)}
-        taps = [[zero] * 4 for _ in range(4)]
-        for j in range(4, 11):
-            rows = [near[d, pl.ds(WIN * t + j, 8, stride=4), :] for d in range(5)]
-            cells = [jnp.where(left, rows[c], rows[c + 1]) for c in range(4)]
-            for r in range(4):
-                if j - 6 - r in hit:
-                    for c in range(4):
-                        taps[r][c] = jnp.where(hit[j - 6 - r], cells[c], taps[r][c])
+        bits = [low_y >= 0.0, (low_y == -1.0) | (low_y == 1.0)]
+        taps = []
+        for c in range(4):
+            cells = []
+            for j in range(4, 11):
+                rows = pl.ds(WIN * t + j, 8, stride=4)
+                cells.append(jnp.where(left, near[c, rows, :], near[c + 1, rows, :]))
+            cells = [jnp.where(bits[0], cells[k + 2], cells[k]) for k in range(5)]
+            taps.append([jnp.where(bits[1], cells[k + 1], cells[k]) for k in range(4)])
         first = stencil(taps, spline_weights(frac_x), spline_weights(rel_y - low_y))
         pos_y = (7.0 + rel_y) - lens_ratio * first[0]
         start = (32 + lax.rem(lane, 64)).astype(jnp.float32)
         pos_x = (start + off_x) - lens_ratio * first[1]
         low_y = jnp.floor(pos_y)
         low_x = jnp.floor(pos_x)
-        xw = spline_weights(pos_x - low_x)
-        yw = spline_weights(pos_y - low_y)
-        cell_x = jnp.clip(low_x, -8.0, 136.0).astype(jnp.int32)
-        cell_y = jnp.clip(low_y, -8.0, 32.0).astype(jnp.int32)
-        spots = [cell_x + (c - 1) for c in range(4)]
-        inside = [(s >= 0) & (s < 128) for s in spots]
-        xw = [[jnp.where(inside[c], w[c], 0.0) for c in range(4)] for w in xw]
-        spots = [jnp.clip(s, 0, 127) for s in spots]
+        cell_x = jnp.clip(low_x, -8.0, 136.0).astype(jnp.int32) - 1
+        cell_y = jnp.clip(low_y, -8.0, 32.0).astype(jnp.int32) - 1
+        xw = kept(spline_weights(pos_x - low_x), cell_x, 128)
+        yw = kept(spline_weights(pos_y - low_y), cell_y, PATCH_ROWS)
         is_even = lane < 64
-        hit = {v: cell_y == v for v in range(-2, 17)}
-        taps = [[zero] * 4 for _ in range(4)]
-        for j in range(16):
-            ev = even[pl.ds(WIN * t + j, 8, stride=4), :]
-            od = odd[pl.ds(WIN * t + j, 8, stride=4), :]
-            for c in range(4):
-                cell = jnp.where(
-                    is_even,
-                    jnp.take_along_axis(ev, spots[c], axis=1),
-                    jnp.take_along_axis(od, spots[c], axis=1),
+        bits = [(cell_y & b) != 0 for b in (8, 4, 2, 1)]
+        taps = []
+        for c in range(4):
+            spots = jnp.clip(cell_x + c, 0, 127)
+            cells = []
+            for j in range(PATCH_ROWS):
+                rows = pl.ds(WIN * t + j, 8, stride=4)
+                cells.append(
+                    jnp.where(is_even, lane_gather(even[rows, :], spots), lane_gather(odd[rows, :], spots))
                 )
-                for r in range(4):
-                    taps[r][c] = jnp.where(hit[j + 1 - r], cell, taps[r][c])
+            cells = [jnp.where(bits[0], cells[(k + 8) % 16], cells[k]) for k in range(11)]
+            cells = [jnp.where(bits[1], cells[k + 4], cells[k]) for k in range(7)]
+            cells = [jnp.where(bits[2], cells[k + 2], cells[k]) for k in range(5)]
+            taps.append([jnp.where(bits[3], cells[k + 1], cells[k]) for k in range(4)])
         second = stencil(taps, xw, yw)
         hess_yy, hess_xx, hess_xy = first[2], first[3], first[4]
         other_yy, other_xx, other_xy = second[2], second[3], second[4]
@@ -366,7 +408,7 @@
         jacob_ref[3, :, cols] = 1.0 - hess_xx - (other_xy * lensed_xy + other_xx * lensed_xx)
         return carry
 
-    lax.fori_loop(0, OUTER, tile, 0)
+    lax.fori_loop(0, OUTER, tile, 0, unroll=UNROLL)
 
 
 def vmem(shape):

time: 112 us -> 99.7 us (0.89)
  Pallas kernels: 52.5 us -> 39.6 us
    pallas_call x3, Pallas kernels: 52.5 us -> 39.6 us  [call(): pl.pallas_call(kernel, name=name, out_shape=outs, in_specs=[pl.BlockSpec(...]
where the time goes in v2:
time: 99.7 us; the launch traced here: 99.3 us
  blocking collectives  59 us (59%)
  Pallas kernels  39.6 us (40%)
    pallas_call x3, Pallas kernels, call(): pl.pallas_call(kernel, name=name, out_shape=outs, in_specs=[pl.BlockSpec(...  39.6 us
    all_to_all x1, blocking collectives, on_device(): lax.all_to_all(strips, ('plane', 'slab'), split_axis=0, concat_axis=0, ti...  30.8 us
    all_to_all x1, blocking collectives, on_device(): lax.all_to_all(spectra.reshape(SLABS, 32, 128), 'slab', split_axis=0, con...  28.2 us

profile of v2, /device:TPU:1, one launch (start us, length us, event | category | flops | bytes accessed | tf_op | source)
XLA Modules:
  0.0 99.3 jit_solution(7843621261792846917)
XLA Ops:
  0.6 6.6 %rows.1 = f32[2048,128]{1,0:T(8,128)} custom-call(f32[64,4096]{1,0:T(8,128)} %bitcast.10, bf16[256,256]{1,0:T(8,128)(2,1)} %constant.16.clone.weight_ref, f32[2,32,128]{2,1,0:T(8,128)} %constant.17.clone.turn_ref), custom_call_target="tpu_custom_call" | custom-call | tf_op jit(solution)/shard_map/rows/pallas_call | solution.py:419
  7.2 28.2 %all_to_all.10.in_ref = f32[64,32,128]{2,1,0:T(8,128)} all-to-all(f32[64,32,128]{2,1,0:T(8,128)} %bitcast.9), channel_id=1, replica_groups=mesh['plane'=2,'slab'=64] {'slab'}, dimensions={0} | all-to-all | bytes 2097152 | tf_op jit(solution)/shard_map/all_to_all | solution.py:439
  35.4 9.1 %columns.1 = f32[128,24,128]{2,1,0:T(8,128)} custom-call(f32[64,32,128]{2,1,0:T(8,128)} %all_to_all.10.in_ref, bf16[256,256]{1,0:T(8,128)(2,1)} %constant.18.clone.fwd_ref, f32[2,64,128]{2,1,0:T(8,128)} %constant.19.clone.turn_ref, f32[64,128]{1,0:T(8,128)} %constant.20.clone.wave_ref, bf16[2,3,128,256]{3,2,1,0:T(8,128)(2,1)} %constant.21.clone.inv_ref, ...), custom_call_target="tpu_custom_call" | custom-call | tf_op jit(solution)/shard_map/columns/pallas_call | solution.py:419
  44.5 30.8 %all_to_all.11.in_ref = f32[128,24,128]{2,1,0:T(8,128)} all-to-all(f32[128,24,128]{2,1,0:T(8,128)} %columns.1), channel_id=1, replica_groups=mesh['plane'=2,'slab'=64] {'plane','slab'}, dimensions={0} | all-to-all | bytes 3145728 | tf_op jit(solution)/shard_map/all_to_all | solution.py:447
  75.3 24.0 %rays.1 = (f32[2,8,4096]{2,1,0:T(8,128)}, f32[4,8,4096]{2,1,0:T(8,128)}) custom-call(f32[128,24,128]{2,1,0:T(8,128)} %all_to_all.11.in_ref, bf16[3,128,256]{2,1,0:T(8,128)(2,1)} %constant.23.clone.inv_ref, f32[2,32,128]{2,1,0:T(8,128)} %constant.17.clone.turn_ref, f32[2,8,4096]{2,1,0:T(8,128)} %bitcast.11), custom_call_target="tpu_custom_call" | custom-call | tf_op jit(solution)/shard_map/rays/pallas_call | solution.py:419

commit v3 on v2

--- a/solution.py
+++ b/solution.py
@@ -14,7 +14,6 @@
 SLABS = 64
 PATCH_ROWS = 16
 WIN = 48
-UNROLL = 1
 LEAD = 5
 lens_ratio = 0.5
 screen_modes = 4.0
@@ -202,7 +201,7 @@
         forward_outer(xs, turn_ref, store)
         return carry
 
-    lax.fori_loop(0, 8, group, 0)
+    lax.fori_loop(0, 8, group, 0, unroll=2)
 
     def pair(i, carry):
         spot = pl.ds(pl.multiple_of(128 * i, 128), 128)
@@ -212,7 +211,7 @@
         out_ref[spot, :] = both[:128] + both[128:]
         return carry
 
-    lax.fori_loop(0, 16, pair, 0)
+    lax.fori_loop(0, 16, pair, 0, unroll=8)
 
 
 def columns_kernel(in_ref, fwd_ref, turn_ref, wave_ref, inv_ref, back_ref, out_ref, mid, spec, strips):
@@ -261,7 +260,7 @@
             out_ref[d, 8 * k : 8 * k + 8, :] = jnp.where(lane < 96, strips[d, 8 * k : 8 * k + 8, :], moved)
         return carry
 
-    lax.fori_loop(0, 2 * SLABS, pack, 0, unroll=4)
+    lax.fori_loop(0, 2 * SLABS, pack, 0, unroll=32)
 
 
 def spline_weights(f):
@@ -318,7 +317,7 @@
             mid[spot, :] = fine_dot(block, inv_ref[...])
             return carry
 
-        lax.fori_loop(0, 16, unpack, 0)
+        lax.fori_loop(0, 16, unpack, 0, unroll=8)
 
         def finish(g, carry):
             def load(m):
@@ -350,7 +349,7 @@
                     odd[spot(t), :] = jnp.where(lane < 96, moved[t], moved[(t + 1) % OUTER])
             return carry
 
-        lax.fori_loop(0, WIN // 8, finish, 0)
+        lax.fori_loop(0, WIN // 8, finish, 0, unroll=3)
 
     def tile(t, carry):
         cols = pl.ds(pl.multiple_of(128 * t, 128), 128)
@@ -408,14 +407,14 @@
         jacob_ref[3, :, cols] = 1.0 - hess_xx - (other_xy * lensed_xy + other_xx * lensed_xx)
         return carry
 
-    lax.fori_loop(0, OUTER, tile, 0, unroll=UNROLL)
+    lax.fori_loop(0, OUTER, tile, 0, unroll=4)
 
 
 def vmem(shape):
     return pltpu.VMEM(shape, jnp.float32)
 
 
-def call(kernel, name, args, outs, scratch):
+def call(kernel, name, args, outs, scratch, limit=16):
     return pl.pallas_call(
         kernel,
         name=name,
@@ -423,7 +422,7 @@
         in_specs=[pl.BlockSpec(memory_space=pltpu.VMEM)] * len(args),
         out_specs=jax.tree.map(lambda _: pl.BlockSpec(memory_space=pltpu.VMEM), outs),
         scratch_shapes=scratch,
-        compiler_params=pltpu.CompilerParams(vmem_limit_bytes=60 * 1024 * 1024),
+        compiler_params=pltpu.CompilerParams(vmem_limit_bytes=limit * 1024 * 1024),
     )(*args)
 
 

time: 99.7 us -> 80.8 us (0.81)
  Pallas kernels: 39.6 us -> 18.3 us
  local copies, waits for them, and re-layouts: 0 us -> 2.93 us
    pallas_call x3, Pallas kernels: 39.6 us -> 18.3 us  [call(): pl.pallas_call(kernel, name=name, out_shape=outs, in_specs=[pl.BlockSpec(...]
    unnamed x0 -> x22, local copies, waits for them, and re-layouts: none -> 2.93 us
where the time goes in v3:
time: 80.8 us; the launch traced here: 80.5 us
  blocking collectives  58.5 us (72%)
  Pallas kernels  18.3 us (23%)
  local copies, waits for them, and re-layouts  2.93 us (4%)
    all_to_all x1, blocking collectives, on_device(): lax.all_to_all(strips, ('plane', 'slab'), split_axis=0, concat_axis=0, ti...  30.5 us
    all_to_all x1, blocking collectives, on_device(): lax.all_to_all(spectra.reshape(SLABS, 32, 128), 'slab', split_axis=0, con...  28.1 us
    pallas_call x3, Pallas kernels, call(): pl.pallas_call(kernel, name=name, out_shape=outs, in_specs=[pl.BlockSpec(...  18.3 us
    unnamed x22, local copies, waits for them, and re-layouts  2.93 us

profile of v3, /device:TPU:1, one launch (start us, length us, event | category | flops | bytes accessed | tf_op | source)
XLA Modules:
  0.0 80.5 jit_solution(15046590301556832617)
XLA Ops:
  0.6 0.0 copy-start
  0.6 1.2 %copy-done = f32[1,64,4096]{2,1,0:T(8,128)S(1)} copy-done((f32[1,64,4096]{2,1,0:T(8,128)S(1)}, f32[1,64,4096]{2,1,0:T(8,128)}, u32[]{:S(2)}) %copy-start) | copy-done | bytes 1048600
  1.9 0.0 copy-start.4
  1.9 0.8 copy-done.4
  2.6 0.0 copy-start.8
  2.6 0.9 %copy-done.8 = bf16[256,256]{1,0:T(8,128)(2,1)S(1)} copy-done((bf16[256,256]{1,0:T(8,128)(2,1)S(1)}, bf16[256,256]{1,0:T(8,128)(2,1)}, u32[]{:S(2)}) %copy-start.8) | copy-done | bytes 131096
  3.5 2.0 %rows.1 = f32[2048,128]{1,0:T(8,128)S(1)} custom-call(f32[64,4096]{1,0:T(8,128)S(1)} %bitcast.10, bf16[256,256]{1,0:T(8,128)(2,1)S(1)} %copy-done.8, f32[2,32,128]{2,1,0:T(8,128)S(1)} %copy-done.4), custom_call_target="tpu_custom_call" | custom-call | tf_op jit(solution)/shard_map/rows/pallas_call | solution.py:418
  5.5 0.0 copy-start.1
  5.5 0.0 copy-start.6
  5.5 0.0 copy-start.7
  5.5 0.0 copy-start.9
  5.5 0.0 copy-start.10
  5.6 28.1 %all_to_all.10.in_ref = f32[64,32,128]{2,1,0:T(8,128)S(1)} all-to-all(f32[64,32,128]{2,1,0:T(8,128)S(1)} %bitcast.9), channel_id=1, replica_groups=mesh['plane'=2,'slab'=64] {'slab'}, dimensions={0} | all-to-all | bytes 2097152 | tf_op jit(solution)/shard_map/all_to_all | solution.py:438
  33.6 0.0 copy-done.1
  33.6 0.0 copy-done.6
  33.6 0.0 copy-done.7
  33.6 0.0 copy-done.9
  33.6 0.0 copy-done.10
  33.6 4.6 %columns.1 = f32[128,24,128]{2,1,0:T(8,128)S(1)} custom-call(f32[64,32,128]{2,1,0:T(8,128)S(1)} %all_to_all.10.in_ref, bf16[256,256]{1,0:T(8,128)(2,1)S(1)} %copy-done.7, f32[2,64,128]{2,1,0:T(8,128)S(1)} %copy-done.9, f32[64,128]{1,0:T(8,128)S(1)} %copy-done.10, bf16[2,3,128,256]{3,2,1,0:T(8,128)(2,1)S(1)} %copy-done.1, f32[2,2,64,128]{3,2,1,0:T(8,128)S(1)} %copy-done.6), custom_call_target="tpu_custom_call" | custom-call | tf_op jit(solution)/shard_map/columns/pallas_call | solution.py:418
  38.2 0.0 copy-start.2
  38.2 0.0 copy-start.3
  38.2 0.0 copy-start.5
  38.3 30.5 %all_to_all.11.in_ref = f32[128,24,128]{2,1,0:T(8,128)S(1)} all-to-all(f32[128,24,128]{2,1,0:T(8,128)S(1)} %columns.1), channel_id=1, replica_groups=mesh['plane'=2,'slab'=64] {'plane','slab'}, dimensions={0} | all-to-all | bytes 3145728 | tf_op jit(solution)/shard_map/all_to_all | solution.py:446
  68.8 0.0 copy-done.2
  68.8 0.0 copy-done.3
  68.8 0.0 copy-done.5
  68.8 11.7 %rays.1 = (f32[2,8,4096]{2,1,0:T(8,128)}, f32[4,8,4096]{2,1,0:T(8,128)}) custom-call(f32[128,24,128]{2,1,0:T(8,128)S(1)} %all_to_all.11.in_ref, bf16[3,128,256]{2,1,0:T(8,128)(2,1)S(1)} %copy-done.3, f32[2,32,128]{2,1,0:T(8,128)S(1)} %copy-done.5, f32[2,8,4096]{2,1,0:T(8,128)S(1)} %bitcast.11), custom_call_target="tpu_custom_call" | custom-call | tf_op jit(solution)/shard_map/rays/pallas_call | solution.py:418
Async XLA Ops:
  0.6 1.2 %copy-start = (f32[1,64,4096]{2,1,0:T(8,128)S(1)}, f32[1,64,4096]{2,1,0:T(8,128)}, u32[]{:S(2)}) copy-start(f32[1,64,4096]{2,1,0:T(8,128)} %param.10) | copy-start | bytes 3145732
  1.9 0.8 copy-start.4
  2.6 0.9 %copy-start.8 = (bf16[256,256]{1,0:T(8,128)(2,1)S(1)}, bf16[256,256]{1,0:T(8,128)(2,1)}, u32[]{:S(2)}) copy-start(bf16[256,256]{1,0:T(8,128)(2,1)} %constant.16.clone.weight_ref) | copy-start | bytes 393220
  5.5 28.1 %copy-start.1 = (bf16[2,3,128,256]{3,2,1,0:T(8,128)(2,1)S(1)}, bf16[2,3,128,256]{3,2,1,0:T(8,128)(2,1)}, u32[]{:S(2)}) copy-start(bf16[2,3,128,256]{3,2,1,0:T(8,128)(2,1)} %constant.21.clone.inv_ref) | copy-start | bytes 1179652
  5.5 28.1 %copy-start.6 = (f32[2,2,64,128]{3,2,1,0:T(8,128)S(1)}, f32[2,2,64,128]{3,2,1,0:T(8,128)}, u32[]{:S(2)}) copy-start(f32[2,2,64,128]{3,2,1,0:T(8,128)} %constant.22.clone.back_ref) | copy-start | bytes 393220
  5.5 28.1 %copy-start.7 = (bf16[256,256]{1,0:T(8,128)(2,1)S(1)}, bf16[256,256]{1,0:T(8,128)(2,1)}, u32[]{:S(2)}) copy-start(bf16[256,256]{1,0:T(8,128)(2,1)} %constant.18.clone.fwd_ref) | copy-start | bytes 393220
  5.5 28.1 %copy-start.9 = (f32[2,64,128]{2,1,0:T(8,128)S(1)}, f32[2,64,128]{2,1,0:T(8,128)}, u32[]{:S(2)}) copy-start(f32[2,64,128]{2,1,0:T(8,128)} %constant.19.clone.turn_ref) | copy-start | bytes 196612
  5.5 28.1 %copy-start.10 = (f32[64,128]{1,0:T(8,128)S(1)}, f32[64,128]{1,0:T(8,128)}, u32[]{:S(2)}) copy-start(f32[64,128]{1,0:T(8,128)} %constant.20.clone.wave_ref) | copy-start | bytes 98308
  38.2 30.5 %copy-start.2 = (f32[2,1,1,8,4096]{4,3,2,1,0:T(8,128)S(1)}, f32[2,1,1,8,4096]{4,3,2,1,0:T(8,128)}, u32[]{:S(2)}) copy-start(f32[2,1,1,8,4096]{4,3,2,1,0:T(8,128)} %param.11) | copy-start | bytes 786436
  38.2 30.5 %copy-start.3 = (bf16[3,128,256]{2,1,0:T(8,128)(2,1)S(1)}, bf16[3,128,256]{2,1,0:T(8,128)(2,1)}, u32[]{:S(2)}) copy-start(bf16[3,128,256]{2,1,0:T(8,128)(2,1)} %constant.23.clone.inv_ref) | copy-start | bytes 589828
  38.2 30.5 %copy-start.5 = (f32[2,32,128]{2,1,0:T(8,128)S(1)}, f32[2,32,128]{2,1,0:T(8,128)}, u32[]{:S(2)}) copy-start(f32[2,32,128]{2,1,0:T(8,128)} %constant.17.clone.turn_ref) | copy-start | bytes 98308

commit v4 on v3

--- a/solution.py
+++ b/solution.py
@@ -13,7 +13,9 @@
 OUTER = 32
 SLABS = 64
 PATCH_ROWS = 16
+NEAR_WIN = 40
 WIN = 48
+ROWS_GRANT = 62 * 1024 * 1024
 LEAD = 5
 lens_ratio = 0.5
 screen_modes = 4.0
@@ -45,7 +47,8 @@
     out = {}
     lane = np.arange(128)
     plus, minus = cas_pair(lane, lane, 128)
-    out["row_fwd"] = np.concatenate(parts(np.concatenate([plus.T, minus.T], axis=1), 2), axis=0)
+    both = np.concatenate([plus, minus], axis=0)
+    out["row_fwd"] = np.concatenate(parts(both, 2), axis=1)
     turn = angles(np.arange(OUTER), lane, N)
     out["row_turn"] = f32(np.stack([np.cos(turn), np.sin(turn)]))
     out["row_inv"] = np.stack(parts(0.5 * np.concatenate([plus, -minus], axis=1), 3))
@@ -56,16 +59,21 @@
     out["col_fwd"] = np.concatenate(parts(both, 2), axis=1)
     turn = angles(sixty, np.concatenate([sixty, sixty]), N)
     out["col_turn"] = f32(np.stack([np.cos(turn), np.sin(turn)]))
-    inv, turns = [], []
+    inv, extra, turns = [], [], []
     for p in range(2):
         rows = 32 * p - LEAD + np.arange(WIN)
         plus, minus = cas_pair(sixty, rows, 64)
-        pad = np.zeros((128, 32))
-        inv.append(np.concatenate([np.kron(two, plus), pad, -np.kron(two, minus), pad], axis=1))
-        turn = angles(sixty, np.concatenate([rows, rows, np.zeros(32, rows.dtype)]), N)
-        turns.append(np.stack([np.cos(turn), np.sin(turn)]))
-    out["col_inv"] = np.stack([np.stack(parts(0.5 * table, 3)) for table in inv])
-    out["col_back"] = f32(np.stack(turns))
+        table = 0.5 * np.stack([np.kron(two, plus), -np.kron(two, minus)], axis=1)
+        turn = angles(sixty, np.concatenate([rows, rows]), N)
+        inv.append(np.pad(table, ((0, 0), (0, 0), (0, 32))).reshape(128, 256))
+        for k in range(3):
+            own = slice(32 * k, 32 * k + 32)
+            extra.append(np.pad(table[:, :, own], ((0, 0), (0, 0), (96, 0))).reshape(128, 256))
+            full = np.concatenate([turn, turn[:, own]], axis=1)
+            turns.append(np.stack([np.cos(full), np.sin(full)]))
+    out["col_inv"] = np.stack([np.stack(parts(table, 3)) for table in inv])
+    out["col_extra"] = np.stack([np.stack(parts(table, 3)) for table in extra]).reshape(2, 3, 3, 128, 256)
+    out["col_back"] = f32(np.stack(turns).reshape(2, 3, 2, 64, 128))
     ids = np.arange(64)[:, None] + 64 * np.concatenate([sixty, sixty])[None, :]
     wave = 2.0 * np.pi / N * np.minimum(ids, N - ids)
     out["wave2"] = f32(wave**2)
@@ -180,48 +188,69 @@
     return out
 
 
+def left_of(pieces):
+    a, b, c = (pieces[:, 128 * i : 128 * i + 128] for i in range(3))
+    return [a, b, a, b, a, c]
+
+
+def right_of(w):
+    return [w[0], w[0], w[1], w[1], w[2], w[0]]
+
+
 def fine_dot(x, w):
-    a, b, c = split(x, 3)
-    w0, w1, w2 = w[0], w[1], w[2]
-    left = jnp.concatenate([a, b, a, b, a, c], axis=1)
-    right = jnp.concatenate([w0, w0, w1, w1, w2, w0], axis=0)
-    return jnp.dot(left, right, preferred_element_type=jnp.float32)
-
-
-def rows_kernel(kappa_ref, weight_ref, turn_ref, out_ref, mid):
-    def group(g, carry):
-        rows = pl.ds(pl.multiple_of(8 * g, 8), 8)
-        xs = [kappa_ref[rows, 128 * j : 128 * j + 128] for j in range(OUTER)]
+    left = jnp.concatenate(left_of(jnp.concatenate(split(x, 3), axis=1)), axis=1)
+    return jnp.dot(left, jnp.concatenate(right_of(w), axis=0), preferred_element_type=jnp.float32)
+
+
+def coarse_dot(x, w):
+    left = jnp.concatenate(split(x, 2), axis=1)
+    both = jnp.dot(left, jnp.concatenate([w, w], axis=0), preferred_element_type=jnp.float32)
+    return both[:, :128] + both[:, 128:]
+
+
+def rows_kernel(kappa_hbm, weight_hbm, turn_hbm, out_hbm, out_ref, kappa_ref, weight_ref, turn_ref, mid, sems):
+    def fetch(g):
+        rows = pl.ds(8 * g, 8)
+        return pltpu.make_async_copy(kappa_hbm.at[rows, :], kappa_ref.at[rows, :], sems.at[g])
+
+    def send(i):
+        rows = pl.ds(512 * i, 512)
+        return pltpu.make_async_copy(out_ref.at[rows, :], out_hbm.at[rows, :], sems.at[10 + i])
+
+    turn_copy = pltpu.make_async_copy(turn_hbm, turn_ref, sems.at[8])
+    weight_copy = pltpu.make_async_copy(weight_hbm, weight_ref, sems.at[9])
+    turn_copy.start()
+    for g in range(8):
+        fetch(g).start()
+    weight_copy.start()
+    turn_copy.wait()
+    for g in range(8):
+        fetch(g).wait()
+        xs = [kappa_ref[8 * g : 8 * g + 8, 128 * j : 128 * j + 128] for j in range(OUTER)]
 
         def store(m, re, im):
-            spot = pl.ds(pl.multiple_of(64 * m + 8 * g, 8), 8)
-            mid[spot, 0:128] = re
-            mid[spot, 128:256] = im
+            mid[64 * m + 8 * g : 64 * m + 8 * g + 8, 0:128] = re
+            mid[64 * m + 8 * g : 64 * m + 8 * g + 8, 128:256] = im
 
         forward_outer(xs, turn_ref, store)
-        return carry
-
-    lax.fori_loop(0, 8, group, 0, unroll=2)
-
-    def pair(i, carry):
-        spot = pl.ds(pl.multiple_of(128 * i, 128), 128)
-        left = jnp.concatenate([weight_ref[...]] * 2, axis=1)
-        right = jnp.concatenate(split(mid[spot, :], 2), axis=1)
-        both = lax.dot_general(left, right, (((1,), (1,)), ((), ())), preferred_element_type=jnp.float32)
-        out_ref[spot, :] = both[:128] + both[128:]
-        return carry
-
-    lax.fori_loop(0, 16, pair, 0, unroll=8)
-
-
-def columns_kernel(in_ref, fwd_ref, turn_ref, wave_ref, inv_ref, back_ref, out_ref, mid, spec, strips):
+    weight_copy.wait()
+    for i in range(4):
+        found = coarse_dot(mid[512 * i : 512 * i + 512, :], weight_ref[...])
+        for k in range(4):
+            out_ref[512 * i + 128 * k : 512 * i + 128 * k + 128, :] = jnp.transpose(found[128 * k : 128 * k + 128])
+        send(i).start()
+    for i in range(4):
+        send(i).wait()
+
+
+def columns_kernel(in_ref, fwd_ref, turn_ref, wave_ref, inv_ref, extra_ref, back_ref, out_ref, mids, specs, pieces):
     owner = lax.axis_index("slab")
     base = 2 * lax.div(owner, 4) + 1024 * lax.rem(owner, 4)
     lane = lax.broadcasted_iota(jnp.int32, (8, 128), 1)
     sub8 = lax.broadcasted_iota(jnp.int32, (8, 128), 0)
     screen = (2.0 * math.pi * screen_modes / N) ** 2
 
-    def group(g, carry):
+    def forward(g, mid, spec):
         rows = pl.ds(pl.multiple_of(8 * g, 8), 8)
         xs = [in_ref[s, rows, :] for s in range(SLABS)]
 
@@ -230,10 +259,7 @@
             mid[8 * m : 8 * m + 8, 128:256] = im
 
         forward_outer(xs, turn_ref, store)
-        left = jnp.concatenate(split(mid[...], 2), axis=1)
-        right = jnp.concatenate([fwd_ref[...]] * 2, axis=0)
-        both = jnp.dot(left, right, preferred_element_type=jnp.float32)
-        spec[...] = both[:, :128] + both[:, 128:]
+        spec[...] = coarse_dot(mid[...], fwd_ref[...])
         ids = base + jnp.where(lane >= 64, 1, 0) + 32 * (8 * g + sub8)
         wave = (2.0 * math.pi / N) * jnp.minimum(ids, N - ids).astype(jnp.float32)
         mine = wave * wave + screen
@@ -242,25 +268,33 @@
             if m == 0:
                 factor = jnp.where((ids == 0) & (lane == 0), 0.0, factor)
             spec[8 * m : 8 * m + 8, :] = spec[8 * m : 8 * m + 8, :] * factor
+        for i, piece in enumerate(split(spec[...], 3)):
+            pieces[g, :, 128 * i : 128 * i + 128] = piece
+
+    def forward_pair(i, carry):
+        forward(2 * i, mids.at[0], specs.at[0])
+        forward(2 * i + 1, mids.at[1], specs.at[1])
+        return carry
+
+    lax.fori_loop(0, 2, forward_pair, 0, unroll=2)
+
+    def backward(k, carry):
         for p in range(2):
-            mid[...] = fine_dot(spec[...], inv_ref[p])
+            mid = mids.at[p]
+            left = left_of(pieces[k]) + left_of(pieces[3])
+            right = right_of(inv_ref[p]) + right_of(extra_ref[p, k])
+            mid[...] = jnp.dot(
+                jnp.concatenate(left, axis=1), jnp.concatenate(right, axis=0), preferred_element_type=jnp.float32
+            )
             values = inverse_outer(
-                lambda m: (mid[8 * m : 8 * m + 8, 0:128], mid[8 * m : 8 * m + 8, 128:256]), SLABS, back_ref, p
+                lambda m: (mid[8 * m : 8 * m + 8, 0:128], mid[8 * m : 8 * m + 8, 128:256]), SLABS, back_ref, p, k
             )
+            rows = pl.ds(pl.multiple_of(8 * k, 8), 8)
             for s in range(SLABS):
-                strips[p * SLABS + s, rows, :] = values[s]
+                out_ref[p * SLABS + s, rows, :] = values[s]
         return carry
 
-    lax.fori_loop(0, 4, group, 0)
-
-    def pack(d, carry):
-        last = strips[d, 24:32, :]
-        for k in range(3):
-            moved = last if k == 3 else pltpu.roll(last, (96 - 32 * k) % 128, 1)
-            out_ref[d, 8 * k : 8 * k + 8, :] = jnp.where(lane < 96, strips[d, 8 * k : 8 * k + 8, :], moved)
-        return carry
-
-    lax.fori_loop(0, 2 * SLABS, pack, 0, unroll=32)
+    lax.fori_loop(0, 3, backward, 0, unroll=3)
 
 
 def spline_weights(f):
@@ -301,33 +335,38 @@
     )
 
 
-def rays_kernel(in_ref, inv_ref, turn_ref, off_ref, deflect_ref, jacob_ref, mid, near, even, odd):
+def rays_kernel(
+    in_ref, inv_ref, turn_ref, off_ref, deflect_hbm, jacob_hbm, deflect_ref, jacob_ref, flat, mid, near, even, odd, sems
+):
     lane = lax.broadcasted_iota(jnp.int32, (8, 128), 1)
 
-    for q in range(2):
+    for q, win in enumerate((NEAR_WIN, WIN)):
         def unpack(i, carry):
-            parts = []
+            rows = []
             for d in range(4):
                 got = [in_ref[q * SLABS + 4 * i + d, 8 * k : 8 * k + 8, :] for k in range(3)]
                 moved = [pltpu.roll(got[k], 32 + 32 * k, 1) for k in range(3)]
-                parts += got
-                parts.append(jnp.where(lane < 32, moved[0], jnp.where(lane < 64, moved[1], moved[2])))
-            block = jnp.transpose(jnp.concatenate(parts, axis=0))[: 2 * WIN]
-            spot = pl.ds(pl.multiple_of(2 * WIN * i, 8), 2 * WIN)
-            mid[spot, :] = fine_dot(block, inv_ref[...])
+                rows += got
+                rows.append(jnp.where(lane < 32, moved[0], jnp.where(lane < 64, moved[1], moved[2])))
+            block = jnp.transpose(jnp.concatenate(rows, axis=0))
+            for h in range(2):
+                spot = pl.ds(pl.multiple_of(win * (2 * i + h), 8), win)
+                flat[spot, :] = block[WIN * h : WIN * h + win]
             return carry
 
         lax.fori_loop(0, 16, unpack, 0, unroll=8)
+        for half in (slice(0, 16 * win), slice(16 * win, 32 * win)):
+            mid[half, :] = fine_dot(flat[half, :], inv_ref[...])
 
         def finish(g, carry):
             def load(m):
-                spot = pl.ds(pl.multiple_of(WIN * m + 8 * g, 8), 8)
+                spot = pl.ds(pl.multiple_of(win * m + 8 * g, 8), 8)
                 return mid[spot, 0:128], mid[spot, 128:256]
 
             values = inverse_outer(load, OUTER, turn_ref)
 
             def spot(t):
-                return pl.ds(pl.multiple_of(WIN * t + 8 * g, 8), 8)
+                return pl.ds(pl.multiple_of(win * t + 8 * g, 8), 8)
 
             if q == 0:
                 for t in range(OUTER):
@@ -349,7 +388,7 @@
                     odd[spot(t), :] = jnp.where(lane < 96, moved[t], moved[(t + 1) % OUTER])
             return carry
 
-        lax.fori_loop(0, WIN // 8, finish, 0, unroll=3)
+        lax.fori_loop(0, win // 8, finish, 0, unroll=5 if q == 0 else 3)
 
     def tile(t, carry):
         cols = pl.ds(pl.multiple_of(128 * t, 128), 128)
@@ -364,7 +403,7 @@
         for c in range(4):
             cells = []
             for j in range(4, 11):
-                rows = pl.ds(WIN * t + j, 8, stride=4)
+                rows = pl.ds(NEAR_WIN * t + j, 8, stride=4)
                 cells.append(jnp.where(left, near[c, rows, :], near[c + 1, rows, :]))
             cells = [jnp.where(bits[0], cells[k + 2], cells[k]) for k in range(5)]
             taps.append([jnp.where(bits[1], cells[k + 1], cells[k]) for k in range(4)])
@@ -407,22 +446,40 @@
         jacob_ref[3, :, cols] = 1.0 - hess_xx - (other_xy * lensed_xy + other_xx * lensed_xx)
         return carry
 
-    lax.fori_loop(0, OUTER, tile, 0, unroll=4)
+    def send(k):
+        cols = pl.ds(pl.multiple_of(1024 * k, 1024), 1024)
+        return [
+            pltpu.make_async_copy(ref.at[:, :, cols], hbm.at[:, :, cols], sems.at[i, k])
+            for i, (ref, hbm) in enumerate(((deflect_ref, deflect_hbm), (jacob_ref, jacob_hbm)))
+        ]
+
+    def chunk(k, carry):
+        for t in range(8):
+            tile(8 * k + t, carry)
+        for copy in send(k):
+            copy.start()
+        return carry
+
+    lax.fori_loop(0, 4, chunk, 0)
+    for k in range(4):
+        for copy in send(k):
+            copy.wait()
 
 
 def vmem(shape):
     return pltpu.VMEM(shape, jnp.float32)
 
 
-def call(kernel, name, args, outs, scratch, limit=16):
+def call(kernel, name, args, outs, scratch, ins=None, out_space=pltpu.VMEM, grant=16 * 1024 * 1024):
+    spaces = [pltpu.VMEM] * len(args) if ins is None else ins
     return pl.pallas_call(
         kernel,
         name=name,
         out_shape=outs,
-        in_specs=[pl.BlockSpec(memory_space=pltpu.VMEM)] * len(args),
-        out_specs=jax.tree.map(lambda _: pl.BlockSpec(memory_space=pltpu.VMEM), outs),
+        in_specs=[pl.BlockSpec(memory_space=space) for space in spaces],
+        out_specs=jax.tree.map(lambda _: pl.BlockSpec(memory_space=out_space), outs),
         scratch_shapes=scratch,
-        compiler_params=pltpu.CompilerParams(vmem_limit_bytes=limit * 1024 * 1024),
+        compiler_params=pltpu.CompilerParams(vmem_limit_bytes=grant),
     )(*args)
 
 
@@ -433,15 +490,29 @@
 def on_device(kappa, ray_offsets):
     tab = tables()
     spectra = call(
-        rows_kernel, "rows", (kappa[0], tab["row_fwd"], tab["row_turn"]), shape(2048, 128), [vmem((2048, 256))]
+        rows_kernel,
+        "rows",
+        (kappa[0], tab["row_fwd"], tab["row_turn"]),
+        shape(2048, 128),
+        [
+            vmem((2048, 128)),
+            vmem((64, N)),
+            pltpu.VMEM((256, 256), jnp.bfloat16),
+            vmem((2, OUTER, 128)),
+            vmem((2048, 256)),
+            pltpu.SemaphoreType.DMA((14,)),
+        ],
+        ins=[pltpu.HBM] * 3,
+        out_space=pltpu.HBM,
+        grant=ROWS_GRANT,
     )
     columns = lax.all_to_all(spectra.reshape(SLABS, 32, 128), "slab", split_axis=0, concat_axis=0, tiled=True)
     strips = call(
         columns_kernel,
         "columns",
-        (columns, tab["col_fwd"], tab["col_turn"], tab["wave2"], tab["col_inv"], tab["col_back"]),
+        (columns, tab["col_fwd"], tab["col_turn"], tab["wave2"], tab["col_inv"], tab["col_extra"], tab["col_back"]),
         shape(2 * SLABS, 24, 128),
-        [vmem((512, 256)), vmem((512, 128)), vmem((2 * SLABS, 32, 128))],
+        [vmem((2, 512, 256)), vmem((2, 512, 128)), pltpu.VMEM((4, 512, 384), jnp.bfloat16)],
     )
     windows = lax.all_to_all(strips, ("plane", "slab"), split_axis=0, concat_axis=0, tiled=True)
     deflection, jacobian = call(
@@ -449,7 +520,17 @@
         "rays",
         (windows, tab["row_inv"], tab["row_turn"], ray_offsets[:, 0, 0]),
         (shape(2, 8, N), shape(4, 8, N)),
-        [vmem((OUTER * WIN, 256)), vmem((5, OUTER * WIN, 128)), vmem((OUTER * WIN, 128)), vmem((OUTER * WIN, 128))],
+        [
+            vmem((2, 8, N)),
+            vmem((4, 8, N)),
+            vmem((OUTER * WIN, 128)),
+            vmem((OUTER * WIN, 256)),
+            vmem((5, OUTER * NEAR_WIN, 128)),
+            vmem((OUTER * WIN, 128)),
+            vmem((OUTER * WIN, 128)),
+            pltpu.SemaphoreType.DMA((2, 4)),
+        ],
+        out_space=pltpu.HBM,
     )
     return deflection[:, None, None], jacobian[:, None, None]
 

time: 80.8 us -> 77.5 us (0.959)
  local copies, waits for them, and re-layouts: 2.93 us -> 0.06 us
    unnamed x22 -> x18, local copies, waits for them, and re-layouts: 2.93 us -> 0.06 us
where the time goes in v4:
time: 77.5 us; the launch traced here: 77.3 us
  blocking collectives  58.8 us (76%)
  Pallas kernels  17.7 us (23%)
    all_to_all x1, blocking collectives, on_device(): lax.all_to_all(strips, ('plane', 'slab'), split_axis=0, concat_axis=0, ti...  30.5 us
    all_to_all x1, blocking collectives, on_device(): lax.all_to_all(spectra.reshape(SLABS, 32, 128), 'slab', split_axis=0, con...  28.3 us
    pallas_call x3, Pallas kernels, call(): pl.pallas_call(kernel, name=name, out_shape=outs, in_specs=[pl.BlockSpec(...  17.7 us

profile of v4, /device:TPU:1, one launch (start us, length us, event | category | flops | bytes accessed | tf_op | source)
XLA Modules:
  0.0 77.3 jit_solution(9775434146065765070)
XLA Ops:
  0.6 0.0 copy-start.7
  0.6 0.0 copy-start.8
  0.7 3.1 %rows.1 = f32[2048,128]{1,0:T(8,128)} custom-call(f32[64,4096]{1,0:T(8,128)} %bitcast.11, bf16[256,256]{1,0:T(8,128)(2,1)} %constant.18.clone.weight_hbm, f32[2,32,128]{2,1,0:T(8,128)} %constant.19.clone.turn_hbm.turn_ref), custom_call_target="tpu_custom_call" | custom-call | tf_op jit(solution)/shard_map/rows/pallas_call | solution.py:475
  3.8 0.0 copy-start
  3.8 0.0 copy-start.1
  3.8 0.0 copy-start.2
  3.8 0.0 copy-start.6
  3.9 28.3 %all_to_all.10.in_ref = f32[64,32,128]{2,1,0:T(8,128)S(1)} all-to-all(f32[64,32,128]{2,1,0:T(8,128)} %bitcast.10), channel_id=1, replica_groups=mesh['plane'=2,'slab'=64] {'slab'}, dimensions={0} | all-to-all | bytes 2097152 | tf_op jit(solution)/shard_map/all_to_all | solution.py:509
  32.1 0.0 copy-done.7
  32.1 0.0 copy-done.8
  32.1 0.0 copy-done
  32.1 0.0 copy-done.1
  32.1 0.0 copy-done.2
  32.1 0.0 copy-done.6
  32.2 4.0 %columns.1 = f32[128,24,128]{2,1,0:T(8,128)S(1)} custom-call(f32[64,32,128]{2,1,0:T(8,128)S(1)} %all_to_all.10.in_ref, bf16[256,256]{1,0:T(8,128)(2,1)S(1)} %copy-done.6, f32[2,64,128]{2,1,0:T(8,128)S(1)} %copy-done.7, f32[64,128]{1,0:T(8,128)S(1)} %copy-done.8, bf16[2,3,128,256]{3,2,1,0:T(8,128)(2,1)S(1)} %copy-done.2, ...), custom_call_target="tpu_custom_call" | custom-call | tf_op jit(solution)/shard_map/columns/pallas_call | solution.py:475
  36.2 0.0 copy-start.3
  36.2 0.0 copy-start.4
  36.2 0.0 copy-start.5
  36.2 30.5 %all_to_all.11.in_ref = f32[128,24,128]{2,1,0:T(8,128)S(1)} all-to-all(f32[128,24,128]{2,1,0:T(8,128)S(1)} %columns.1), channel_id=1, replica_groups=mesh['plane'=2,'slab'=64] {'plane','slab'}, dimensions={0} | all-to-all | bytes 3145728 | tf_op jit(solution)/shard_map/all_to_all | solution.py:517
  66.7 0.0 copy-done.3
  66.7 0.0 copy-done.4
  66.7 0.0 copy-done.5
  66.7 10.5 %rays.1 = (f32[2,8,4096]{2,1,0:T(8,128)}, f32[4,8,4096]{2,1,0:T(8,128)}) custom-call(f32[128,24,128]{2,1,0:T(8,128)S(1)} %all_to_all.11.in_ref, bf16[3,128,256]{2,1,0:T(8,128)(2,1)S(1)} %copy-done.4, f32[2,32,128]{2,1,0:T(8,128)S(1)} %copy-done.5, f32[2,8,4096]{2,1,0:T(8,128)S(1)} %bitcast.9), custom_call_target="tpu_custom_call" | custom-call | tf_op jit(solution)/shard_map/rays/pallas_call | solution.py:475
Async XLA Ops:
  0.6 31.5 %copy-start.7 = (f32[2,64,128]{2,1,0:T(8,128)S(1)}, f32[2,64,128]{2,1,0:T(8,128)}, u32[]{:S(2)}) copy-start(f32[2,64,128]{2,1,0:T(8,128)} %constant.21.clone.turn_ref) | copy-start | bytes 196612
  0.6 31.5 %copy-start.8 = (f32[64,128]{1,0:T(8,128)S(1)}, f32[64,128]{1,0:T(8,128)}, u32[]{:S(2)}) copy-start(f32[64,128]{1,0:T(8,128)} %constant.22.clone.wave_ref) | copy-start | bytes 98308
  3.8 28.3 %copy-start = (bf16[2,3,3,128,256]{4,3,2,1,0:T(8,128)(2,1)S(1)}, bf16[2,3,3,128,256]{4,3,2,1,0:T(8,128)(2,1)}, u32[]{:S(2)}) copy-start(bf16[2,3,3,128,256]{4,3,2,1,0:T(8,128)(2,1)} %constant.24.clone.extra_ref) | copy-start | bytes 3538948
  3.8 28.3 %copy-start.1 = (f32[2,3,2,64,128]{4,3,2,1,0:T(8,128)S(1)}, f32[2,3,2,64,128]{4,3,2,1,0:T(8,128)}, u32[]{:S(2)}) copy-start(f32[2,3,2,64,128]{4,3,2,1,0:T(8,128)} %constant.25.clone.back_ref) | copy-start | bytes 1179652
  3.8 28.3 %copy-start.2 = (bf16[2,3,128,256]{3,2,1,0:T(8,128)(2,1)S(1)}, bf16[2,3,128,256]{3,2,1,0:T(8,128)(2,1)}, u32[]{:S(2)}) copy-start(bf16[2,3,128,256]{3,2,1,0:T(8,128)(2,1)} %constant.23.clone.inv_ref) | copy-start | bytes 1179652
  3.8 28.3 %copy-start.6 = (bf16[256,256]{1,0:T(8,128)(2,1)S(1)}, bf16[256,256]{1,0:T(8,128)(2,1)}, u32[]{:S(2)}) copy-start(bf16[256,256]{1,0:T(8,128)(2,1)} %constant.20.clone.fwd_ref) | copy-start | bytes 393220
  36.2 30.5 %copy-start.3 = (f32[2,1,1,8,4096]{4,3,2,1,0:T(8,128)S(1)}, f32[2,1,1,8,4096]{4,3,2,1,0:T(8,128)}, u32[]{:S(2)}) copy-start(f32[2,1,1,8,4096]{4,3,2,1,0:T(8,128)} %param.12) | copy-start | bytes 786436
  36.2 30.5 %copy-start.4 = (bf16[3,128,256]{2,1,0:T(8,128)(2,1)S(1)}, bf16[3,128,256]{2,1,0:T(8,128)(2,1)}, u32[]{:S(2)}) copy-start(bf16[3,128,256]{2,1,0:T(8,128)(2,1)} %constant.26.clone.inv_ref) | copy-start | bytes 589828
  36.2 30.5 %copy-start.5 = (f32[2,32,128]{2,1,0:T(8,128)S(1)}, f32[2,32,128]{2,1,0:T(8,128)}, u32[]{:S(2)}) copy-start(f32[2,32,128]{2,1,0:T(8,128)} %constant.19.clone.turn_hbm.turn_ref) | copy-start | bytes 98308

commit v5 on v4

--- a/solution.py
+++ b/solution.py
@@ -16,6 +16,8 @@
 NEAR_WIN = 40
 WIN = 48
 ROWS_GRANT = 62 * 1024 * 1024
+NEAR_STEP = 4
+FAR_STEP = 4
 LEAD = 5
 lens_ratio = 0.5
 screen_modes = 4.0
@@ -317,12 +319,16 @@
     flat = [dot4(xw[0], row) for row in rows]
     slope = [dot4(xw[1], row) for row in rows]
     curve = [dot4(xw[2], row) for row in rows]
+    return across_rows(flat, slope, curve, yw)
+
+
+def across_rows(flat, slope, curve, yw):
     return dot4(yw[1], flat), dot4(yw[0], slope), dot4(yw[2], flat), dot4(yw[0], curve), dot4(yw[1], slope)
 
 
-def kept(weights, first, count):
-    inside = [(first + c >= 0) & (first + c < count) for c in range(4)]
-    return [[jnp.where(inside[c], w[c], 0.0) for c in range(4)] for w in weights]
+def kept(weights, cells, count):
+    inside = [(cell >= 0) & (cell < count) for cell in cells]
+    return [[jnp.where(inside[c], w[c], 0.0) for c in range(len(cells))] for w in weights]
 
 
 def lane_gather(values, spots):
@@ -336,7 +342,7 @@
 
 
 def rays_kernel(
-    in_ref, inv_ref, turn_ref, off_ref, deflect_hbm, jacob_hbm, deflect_ref, jacob_ref, flat, mid, near, even, odd, sems
+    in_ref, inv_ref, turn_ref, off_ref, deflect_hbm, jacob_hbm, deflect_ref, jacob_ref, flat, mid, near, even, odd, first, pos, halves, sems
 ):
     lane = lax.broadcasted_iota(jnp.int32, (8, 128), 1)
 
@@ -390,7 +396,12 @@
 
         lax.fori_loop(0, win // 8, finish, 0, unroll=5 if q == 0 else 3)
 
-    def tile(t, carry):
+    low_half = lane < 64
+
+    def spot8(t):
+        return pl.ds(pl.multiple_of(8 * t, 8), 8)
+
+    def near_tile(t):
         cols = pl.ds(pl.multiple_of(128 * t, 128), 128)
         off_y = off_ref[0, :, cols]
         off_x = off_ref[1, :, cols]
@@ -407,44 +418,73 @@
                 cells.append(jnp.where(left, near[c, rows, :], near[c + 1, rows, :]))
             cells = [jnp.where(bits[0], cells[k + 2], cells[k]) for k in range(5)]
             taps.append([jnp.where(bits[1], cells[k + 1], cells[k]) for k in range(4)])
-        first = stencil(taps, spline_weights(frac_x), spline_weights(rel_y - low_y))
-        pos_y = (7.0 + rel_y) - lens_ratio * first[0]
+        found = stencil(taps, spline_weights(frac_x), spline_weights(rel_y - low_y))
+        pos_y = (7.0 + rel_y) - lens_ratio * found[0]
         start = (32 + lax.rem(lane, 64)).astype(jnp.float32)
-        pos_x = (start + off_x) - lens_ratio * first[1]
+        pos_x = (start + off_x) - lens_ratio * found[1]
+        for i in range(5):
+            first[i, spot8(t), :] = found[i]
+        pos[0, spot8(t), :] = pos_x
+        pos[1, spot8(t), :] = pos_y
+        pos[2, spot8(t), :] = pltpu.roll(pos_x, 64, 1)
+        pos[3, spot8(t), :] = pltpu.roll(pos_y, 64, 1)
+
+    def far_tile(t):
+        for side, (source, mask) in enumerate(((even, low_half), (odd, ~low_half))):
+            block_x = jnp.where(mask, pos[0, spot8(t), :], pos[2, spot8(t), :])
+            block_y = jnp.where(mask, pos[1, spot8(t), :], pos[3, spot8(t), :])
+            low_x = jnp.floor(block_x)
+            cell_x = jnp.clip(low_x, -8.0, 136.0).astype(jnp.int32) - jnp.where(low_half, 1, 0)
+            cell_y = jnp.clip(jnp.floor(block_y), -8.0, 32.0).astype(jnp.int32) - 1
+            weights = spline_weights(block_x - low_x)
+            weights = [[jnp.where(low_half, w[2 * c], w[2 * c + 1]) for c in range(2)] for w in weights]
+            spots = [cell_x, cell_x + 2]
+            xw = kept(weights, spots, 128)
+            bits = [(cell_y & b) != 0 for b in (8, 4, 2, 1)]
+            taps = []
+            for c in range(2):
+                spot = jnp.clip(spots[c], 0, 127)
+                cells = []
+                for j in range(PATCH_ROWS):
+                    cells.append(lane_gather(source[pl.ds(WIN * t + j, 8, stride=4), :], spot))
+                cells = [jnp.where(bits[0], cells[(k + 8) % 16], cells[k]) for k in range(11)]
+                cells = [jnp.where(bits[1], cells[k + 4], cells[k]) for k in range(7)]
+                cells = [jnp.where(bits[2], cells[k + 2], cells[k]) for k in range(5)]
+                taps.append([jnp.where(bits[3], cells[k + 1], cells[k]) for k in range(4)])
+            for i, w in enumerate(xw):
+                for r in range(4):
+                    halves[side, 4 * i + r, spot8(t), :] = w[0] * taps[0][r] + w[1] * taps[1][r]
+
+    def last_tile(t):
+        cols = pl.ds(pl.multiple_of(128 * t, 128), 128)
+        across = []
+        for i in range(12):
+            e, o = halves[0, i, spot8(t), :], halves[1, i, spot8(t), :]
+            across.append(jnp.where(low_half, e, o) + pltpu.roll(jnp.where(low_half, o, e), 64, 1))
+        pos_y = pos[1, spot8(t), :]
         low_y = jnp.floor(pos_y)
-        low_x = jnp.floor(pos_x)
-        cell_x = jnp.clip(low_x, -8.0, 136.0).astype(jnp.int32) - 1
         cell_y = jnp.clip(low_y, -8.0, 32.0).astype(jnp.int32) - 1
-        xw = kept(spline_weights(pos_x - low_x), cell_x, 128)
-        yw = kept(spline_weights(pos_y - low_y), cell_y, PATCH_ROWS)
-        is_even = lane < 64
-        bits = [(cell_y & b) != 0 for b in (8, 4, 2, 1)]
-        taps = []
-        for c in range(4):
-            spots = jnp.clip(cell_x + c, 0, 127)
-            cells = []
-            for j in range(PATCH_ROWS):
-                rows = pl.ds(WIN * t + j, 8, stride=4)
-                cells.append(
-                    jnp.where(is_even, lane_gather(even[rows, :], spots), lane_gather(odd[rows, :], spots))
-                )
-            cells = [jnp.where(bits[0], cells[(k + 8) % 16], cells[k]) for k in range(11)]
-            cells = [jnp.where(bits[1], cells[k + 4], cells[k]) for k in range(7)]
-            cells = [jnp.where(bits[2], cells[k + 2], cells[k]) for k in range(5)]
-            taps.append([jnp.where(bits[3], cells[k + 1], cells[k]) for k in range(4)])
-        second = stencil(taps, xw, yw)
-        hess_yy, hess_xx, hess_xy = first[2], first[3], first[4]
+        yw = kept(spline_weights(pos_y - low_y), [cell_y + c for c in range(4)], PATCH_ROWS)
+        second = across_rows(across[0:4], across[4:8], across[8:12], yw)
+        slope_y, slope_x, hess_yy, hess_xx, hess_xy = [first[i, spot8(t), :] for i in range(5)]
         other_yy, other_xx, other_xy = second[2], second[3], second[4]
         lensed_yy = 1.0 - lens_ratio * hess_yy
         lensed_xx = 1.0 - lens_ratio * hess_xx
         lensed_xy = -lens_ratio * hess_xy
-        deflect_ref[0, :, cols] = first[0] + second[0]
-        deflect_ref[1, :, cols] = first[1] + second[1]
+        deflect_ref[0, :, cols] = slope_y + second[0]
+        deflect_ref[1, :, cols] = slope_x + second[1]
         jacob_ref[0, :, cols] = 1.0 - hess_yy - (other_yy * lensed_yy + other_xy * lensed_xy)
         jacob_ref[1, :, cols] = -hess_xy - (other_yy * lensed_xy + other_xy * lensed_xx)
         jacob_ref[2, :, cols] = -hess_xy - (other_xy * lensed_yy + other_xx * lensed_xy)
         jacob_ref[3, :, cols] = 1.0 - hess_xx - (other_xy * lensed_xy + other_xx * lensed_xx)
-        return carry
+
+    def several(step, count):
+        def body(i, carry):
+            for k in range(count):
+                step(count * i + k)
+            return carry
+
+        return body
 
     def send(k):
         cols = pl.ds(pl.multiple_of(1024 * k, 1024), 1024)
@@ -453,14 +493,32 @@
             for i, (ref, hbm) in enumerate(((deflect_ref, deflect_hbm), (jacob_ref, jacob_hbm)))
         ]
 
-    def chunk(k, carry):
-        for t in range(8):
-            tile(8 * k + t, carry)
-        for copy in send(k):
-            copy.start()
+    def body(i, carry):
+        for k in range(FAR_STEP):
+            last_tile(FAR_STEP * i - FAR_STEP + k)
+            far_tile(FAR_STEP * i + k)
+            near_tile(FAR_STEP * i + FAR_STEP + k)
+
+        @pl.when(lax.rem(i, 2) == 0)
+        def _():
+            for copy in send(lax.div(i, 2) - 1):
+                copy.start()
+
         return carry
 
-    lax.fori_loop(0, 4, chunk, 0)
+    for k in range(FAR_STEP):
+        near_tile(k)
+    for k in range(FAR_STEP):
+        far_tile(k)
+        near_tile(FAR_STEP + k)
+    lax.fori_loop(1, OUTER // FAR_STEP - 1, body, 0)
+    for k in range(FAR_STEP):
+        last_tile(OUTER - 2 * FAR_STEP + k)
+        far_tile(OUTER - FAR_STEP + k)
+    for k in range(FAR_STEP):
+        last_tile(OUTER - FAR_STEP + k)
+    for copy in send(3):
+        copy.start()
     for k in range(4):
         for copy in send(k):
             copy.wait()
@@ -528,8 +586,12 @@
             vmem((5, OUTER * NEAR_WIN, 128)),
             vmem((OUTER * WIN, 128)),
             vmem((OUTER * WIN, 128)),
+            vmem((5, 8 * OUTER, 128)),
+            vmem((4, 8 * OUTER, 128)),
+            vmem((2, 12, 8 * OUTER, 128)),
             pltpu.SemaphoreType.DMA((2, 4)),
         ],
+        grant=20 * 1024 * 1024,
         out_space=pltpu.HBM,
     )
     return deflection[:, None, None], jacobian[:, None, None]

time: 77.5 us -> 76.1 us (0.982)
  Pallas kernels: 17.7 us -> 16.2 us
    pallas_call x3, Pallas kernels: 17.7 us -> 16.2 us  [call(): pl.pallas_call(kernel, name=name, out_shape=outs, in_specs=[pl.BlockSpec(...]
where the time goes in v5:
time: 76.1 us; the launch traced here: 75.8 us
  blocking collectives  58.8 us (77%)
  Pallas kernels  16.2 us (21%)
    all_to_all x1, blocking collectives, on_device(): lax.all_to_all(strips, ('plane', 'slab'), split_axis=0, concat_axis=0, ti...  30.5 us
    all_to_all x1, blocking collectives, on_device(): lax.all_to_all(spectra.reshape(SLABS, 32, 128), 'slab', split_axis=0, con...  28.3 us
    pallas_call x3, Pallas kernels, call(): pl.pallas_call(kernel, name=name, out_shape=outs, in_specs=[pl.BlockSpec(...  16.2 us

profile of v5, /device:TPU:1, one launch (start us, length us, event | category | flops | bytes accessed | tf_op | source)
XLA Modules:
  0.0 75.8 jit_solution(14303998322025443303)
XLA Ops:
  0.6 0.0 copy-start.7
  0.6 0.0 copy-start.8
  0.7 3.1 %rows.1 = f32[2048,128]{1,0:T(8,128)} custom-call(f32[64,4096]{1,0:T(8,128)} %bitcast.11, bf16[256,256]{1,0:T(8,128)(2,1)} %constant.18.clone.weight_hbm, f32[2,32,128]{2,1,0:T(8,128)} %constant.19.clone.turn_hbm.turn_ref), custom_call_target="tpu_custom_call" | custom-call | tf_op jit(solution)/shard_map/rows/pallas_call | solution.py:533
  3.8 0.0 copy-start
  3.8 0.0 copy-start.1
  3.8 0.0 copy-start.2
  3.8 0.0 copy-start.6
  3.9 28.3 %all_to_all.10.in_ref = f32[64,32,128]{2,1,0:T(8,128)S(1)} all-to-all(f32[64,32,128]{2,1,0:T(8,128)} %bitcast.10), channel_id=1, replica_groups=mesh['plane'=2,'slab'=64] {'slab'}, dimensions={0} | all-to-all | bytes 2097152 | tf_op jit(solution)/shard_map/all_to_all | solution.py:567
  32.1 0.0 copy-done.7
  32.1 0.0 copy-done.8
  32.1 0.0 copy-done
  32.1 0.0 copy-done.1
  32.1 0.0 copy-done.2
  32.1 0.0 copy-done.6
  32.2 4.0 %columns.1 = f32[128,24,128]{2,1,0:T(8,128)S(1)} custom-call(f32[64,32,128]{2,1,0:T(8,128)S(1)} %all_to_all.10.in_ref, bf16[256,256]{1,0:T(8,128)(2,1)S(1)} %copy-done.6, f32[2,64,128]{2,1,0:T(8,128)S(1)} %copy-done.7, f32[64,128]{1,0:T(8,128)S(1)} %copy-done.8, bf16[2,3,128,256]{3,2,1,0:T(8,128)(2,1)S(1)} %copy-done.2, ...), custom_call_target="tpu_custom_call" | custom-call | tf_op jit(solution)/shard_map/columns/pallas_call | solution.py:533
  36.2 0.0 copy-start.3
  36.2 0.0 copy-start.4
  36.2 0.0 copy-start.5
  36.2 30.5 %all_to_all.11.in_ref = f32[128,24,128]{2,1,0:T(8,128)S(1)} all-to-all(f32[128,24,128]{2,1,0:T(8,128)S(1)} %columns.1), channel_id=1, replica_groups=mesh['plane'=2,'slab'=64] {'plane','slab'}, dimensions={0} | all-to-all | bytes 3145728 | tf_op jit(solution)/shard_map/all_to_all | solution.py:575
  66.7 0.0 copy-done.3
  66.7 0.0 copy-done.4
  66.7 0.0 copy-done.5
  66.7 9.1 %rays.1 = (f32[2,8,4096]{2,1,0:T(8,128)}, f32[4,8,4096]{2,1,0:T(8,128)}) custom-call(f32[128,24,128]{2,1,0:T(8,128)S(1)} %all_to_all.11.in_ref, bf16[3,128,256]{2,1,0:T(8,128)(2,1)S(1)} %copy-done.4, f32[2,32,128]{2,1,0:T(8,128)S(1)} %copy-done.5, f32[2,8,4096]{2,1,0:T(8,128)S(1)} %bitcast.9), custom_call_target="tpu_custom_call" | custom-call | tf_op jit(solution)/shard_map/rays/pallas_call | solution.py:533
Async XLA Ops:
  0.6 31.5 %copy-start.7 = (f32[2,64,128]{2,1,0:T(8,128)S(1)}, f32[2,64,128]{2,1,0:T(8,128)}, u32[]{:S(2)}) copy-start(f32[2,64,128]{2,1,0:T(8,128)} %constant.21.clone.turn_ref) | copy-start | bytes 196612
  0.6 31.5 %copy-start.8 = (f32[64,128]{1,0:T(8,128)S(1)}, f32[64,128]{1,0:T(8,128)}, u32[]{:S(2)}) copy-start(f32[64,128]{1,0:T(8,128)} %constant.22.clone.wave_ref) | copy-start | bytes 98308
  3.8 28.3 %copy-start = (bf16[2,3,3,128,256]{4,3,2,1,0:T(8,128)(2,1)S(1)}, bf16[2,3,3,128,256]{4,3,2,1,0:T(8,128)(2,1)}, u32[]{:S(2)}) copy-start(bf16[2,3,3,128,256]{4,3,2,1,0:T(8,128)(2,1)} %constant.24.clone.extra_ref) | copy-start | bytes 3538948
  3.8 28.3 %copy-start.1 = (f32[2,3,2,64,128]{4,3,2,1,0:T(8,128)S(1)}, f32[2,3,2,64,128]{4,3,2,1,0:T(8,128)}, u32[]{:S(2)}) copy-start(f32[2,3,2,64,128]{4,3,2,1,0:T(8,128)} %constant.25.clone.back_ref) | copy-start | bytes 1179652
  3.8 28.3 %copy-start.2 = (bf16[2,3,128,256]{3,2,1,0:T(8,128)(2,1)S(1)}, bf16[2,3,128,256]{3,2,1,0:T(8,128)(2,1)}, u32[]{:S(2)}) copy-start(bf16[2,3,128,256]{3,2,1,0:T(8,128)(2,1)} %constant.23.clone.inv_ref) | copy-start | bytes 1179652
  3.8 28.3 %copy-start.6 = (bf16[256,256]{1,0:T(8,128)(2,1)S(1)}, bf16[256,256]{1,0:T(8,128)(2,1)}, u32[]{:S(2)}) copy-start(bf16[256,256]{1,0:T(8,128)(2,1)} %constant.20.clone.fwd_ref) | copy-start | bytes 393220
  36.2 30.5 %copy-start.3 = (f32[2,1,1,8,4096]{4,3,2,1,0:T(8,128)S(1)}, f32[2,1,1,8,4096]{4,3,2,1,0:T(8,128)}, u32[]{:S(2)}) copy-start(f32[2,1,1,8,4096]{4,3,2,1,0:T(8,128)} %param.12) | copy-start | bytes 786436
  36.2 30.5 %copy-start.4 = (bf16[3,128,256]{2,1,0:T(8,128)(2,1)S(1)}, bf16[3,128,256]{2,1,0:T(8,128)(2,1)}, u32[]{:S(2)}) copy-start(bf16[3,128,256]{2,1,0:T(8,128)(2,1)} %constant.26.clone.inv_ref) | copy-start | bytes 589828
  36.2 30.5 %copy-start.5 = (f32[2,32,128]{2,1,0:T(8,128)S(1)}, f32[2,32,128]{2,1,0:T(8,128)}, u32[]{:S(2)}) copy-start(f32[2,32,128]{2,1,0:T(8,128)} %constant.19.clone.turn_hbm.turn_ref) | copy-start | bytes 98308

commit v6 on v5

--- a/solution.py
+++ b/solution.py
@@ -61,20 +61,18 @@
     out["col_fwd"] = np.concatenate(parts(both, 2), axis=1)
     turn = angles(sixty, np.concatenate([sixty, sixty]), N)
     out["col_turn"] = f32(np.stack([np.cos(turn), np.sin(turn)]))
-    inv, extra, turns = [], [], []
+    inv, turns = [], []
     for p in range(2):
         rows = 32 * p - LEAD + np.arange(WIN)
         plus, minus = cas_pair(sixty, rows, 64)
         table = 0.5 * np.stack([np.kron(two, plus), -np.kron(two, minus)], axis=1)
         turn = angles(sixty, np.concatenate([rows, rows]), N)
-        inv.append(np.pad(table, ((0, 0), (0, 0), (0, 32))).reshape(128, 256))
         for k in range(3):
             own = slice(32 * k, 32 * k + 32)
-            extra.append(np.pad(table[:, :, own], ((0, 0), (0, 0), (96, 0))).reshape(128, 256))
+            inv.append(np.concatenate([table, table[:, :, own]], axis=2).reshape(128, 256))
             full = np.concatenate([turn, turn[:, own]], axis=1)
             turns.append(np.stack([np.cos(full), np.sin(full)]))
-    out["col_inv"] = np.stack([np.stack(parts(table, 3)) for table in inv])
-    out["col_extra"] = np.stack([np.stack(parts(table, 3)) for table in extra]).reshape(2, 3, 3, 128, 256)
+    out["col_inv"] = np.stack([np.stack(parts(table, 3)) for table in inv]).reshape(2, 3, 3, 128, 256)
     out["col_back"] = f32(np.stack(turns).reshape(2, 3, 2, 64, 128))
     ids = np.arange(64)[:, None] + 64 * np.concatenate([sixty, sixty])[None, :]
     wave = 2.0 * np.pi / N * np.minimum(ids, N - ids)
@@ -245,7 +243,7 @@
         send(i).wait()
 
 
-def columns_kernel(in_ref, fwd_ref, turn_ref, wave_ref, inv_ref, extra_ref, back_ref, out_ref, mids, specs, pieces):
+def columns_kernel(in_ref, fwd_ref, turn_ref, wave_ref, inv_ref, back_ref, out_ref, mids, specs, pieces):
     owner = lax.axis_index("slab")
     base = 2 * lax.div(owner, 4) + 1024 * lax.rem(owner, 4)
     lane = lax.broadcasted_iota(jnp.int32, (8, 128), 1)
@@ -281,10 +279,14 @@
     lax.fori_loop(0, 2, forward_pair, 0, unroll=2)
 
     def backward(k, carry):
+        slot = lax.rem(lax.broadcasted_iota(jnp.int32, (128, 256), 1), 128) // 32
+        given = jnp.where(slot == k, 1.0, 0.0)
+        taken, given = (1.0 - given).astype(jnp.bfloat16), given.astype(jnp.bfloat16)
         for p in range(2):
             mid = mids.at[p]
             left = left_of(pieces[k]) + left_of(pieces[3])
-            right = right_of(inv_ref[p]) + right_of(extra_ref[p, k])
+            right = right_of([inv_ref[p, k, i] * taken for i in range(3)])
+            right += right_of([inv_ref[p, k, i] * given for i in range(3)])
             mid[...] = jnp.dot(
                 jnp.concatenate(left, axis=1), jnp.concatenate(right, axis=0), preferred_element_type=jnp.float32
             )
@@ -346,21 +348,25 @@
 ):
     lane = lax.broadcasted_iota(jnp.int32, (8, 128), 1)
 
+    row_group = lax.rem(lax.broadcasted_iota(jnp.int32, (32, 128), 1), 32) // 8
+
     for q, win in enumerate((NEAR_WIN, WIN)):
         def unpack(i, carry):
             rows = []
             for d in range(4):
                 got = [in_ref[q * SLABS + 4 * i + d, 8 * k : 8 * k + 8, :] for k in range(3)]
-                moved = [pltpu.roll(got[k], 32 + 32 * k, 1) for k in range(3)]
                 rows += got
-                rows.append(jnp.where(lane < 32, moved[0], jnp.where(lane < 64, moved[1], moved[2])))
+                rows.append(jnp.where(lane < 32, got[0], jnp.where(lane < 64, got[1], got[2])))
             block = jnp.transpose(jnp.concatenate(rows, axis=0))
+            block = jnp.concatenate(
+                [jnp.where(row_group == k, block[96:128], block[32 * k : 32 * k + 32]) for k in range(3)], axis=0
+            )
             for h in range(2):
                 spot = pl.ds(pl.multiple_of(win * (2 * i + h), 8), win)
                 flat[spot, :] = block[WIN * h : WIN * h + win]
             return carry
 
-        lax.fori_loop(0, 16, unpack, 0, unroll=8)
+        lax.fori_loop(0, 16, unpack, 0, unroll=16)
         for half in (slice(0, 16 * win), slice(16 * win, 32 * win)):
             mid[half, :] = fine_dot(flat[half, :], inv_ref[...])
 
@@ -568,7 +574,7 @@
     strips = call(
         columns_kernel,
         "columns",
-        (columns, tab["col_fwd"], tab["col_turn"], tab["wave2"], tab["col_inv"], tab["col_extra"], tab["col_back"]),
+        (columns, tab["col_fwd"], tab["col_turn"], tab["wave2"], tab["col_inv"], tab["col_back"]),
         shape(2 * SLABS, 24, 128),
         [vmem((2, 512, 256)), vmem((2, 512, 128)), pltpu.VMEM((4, 512, 384), jnp.bfloat16)],
     )
@@ -583,7 +589,7 @@
             vmem((4, 8, N)),
             vmem((OUTER * WIN, 128)),
             vmem((OUTER * WIN, 256)),
-            vmem((5, OUTER * NEAR_WIN, 128)),
+            vmem((5, OUTER * NEAR_WIN + 8, 128)),
             vmem((OUTER * WIN, 128)),
             vmem((OUTER * WIN, 128)),
             vmem((5, 8 * OUTER, 128)),

time: 76.1 us -> 74.5 us (0.979)
  Pallas kernels: 16.2 us -> 14.7 us
    pallas_call x3, Pallas kernels: 16.2 us -> 14.7 us  [call(): pl.pallas_call(kernel, name=name, out_shape=outs, in_specs=[pl.BlockSpec(...]
where the time goes in v6:
time: 74.5 us; the launch traced here: 74.3 us
  blocking collectives  58.7 us (79%)
  Pallas kernels  14.7 us (20%)
    all_to_all x1, blocking collectives, on_device(): lax.all_to_all(strips, ('plane', 'slab'), split_axis=0, concat_axis=0, ti...  30.5 us
    all_to_all x1, blocking collectives, on_device(): lax.all_to_all(spectra.reshape(SLABS, 32, 128), 'slab', split_axis=0, con...  28.3 us
    pallas_call x3, Pallas kernels, call(): pl.pallas_call(kernel, name=name, out_shape=outs, in_specs=[pl.BlockSpec(...  14.7 us

profile of v6, /device:TPU:1, one launch (start us, length us, event | category | flops | bytes accessed | tf_op | source)
XLA Modules:
  0.0 74.3 jit_solution(4704476675327354599)
XLA Ops:
  0.6 3.1 %rows.1 = f32[2048,128]{1,0:T(8,128)} custom-call(f32[64,4096]{1,0:T(8,128)} %bitcast.11, bf16[256,256]{1,0:T(8,128)(2,1)} %constant.16.clone.weight_hbm, f32[2,32,128]{2,1,0:T(8,128)} %constant.17.clone.turn_hbm.turn_ref), custom_call_target="tpu_custom_call" | custom-call | tf_op jit(solution)/shard_map/rows/pallas_call | solution.py:539
  3.8 0.0 copy-start
  3.8 0.0 copy-start.1
  3.8 0.0 copy-start.5
  3.8 0.0 copy-start.6
  3.8 0.0 copy-start.7
  3.8 28.3 %all_to_all.10.in_ref = f32[64,32,128]{2,1,0:T(8,128)S(1)} all-to-all(f32[64,32,128]{2,1,0:T(8,128)} %bitcast.10), channel_id=1, replica_groups=mesh['plane'=2,'slab'=64] {'slab'}, dimensions={0} | all-to-all | bytes 2097152 | tf_op jit(solution)/shard_map/all_to_all | solution.py:573
  32.1 0.0 copy-done
  32.1 0.0 copy-done.1
  32.1 0.0 copy-done.5
  32.1 0.0 copy-done.6
  32.1 0.0 copy-done.7
  32.1 4.2 %columns.1 = f32[128,24,128]{2,1,0:T(8,128)S(1)} custom-call(f32[64,32,128]{2,1,0:T(8,128)S(1)} %all_to_all.10.in_ref, bf16[256,256]{1,0:T(8,128)(2,1)S(1)} %copy-done.5, f32[2,64,128]{2,1,0:T(8,128)S(1)} %copy-done.6, f32[64,128]{1,0:T(8,128)S(1)} %copy-done.7, bf16[2,3,3,128,256]{4,3,2,1,0:T(8,128)(2,1)S(1)} %copy-done, f32[2,3,2,64,128]{4,3,2,1,0:T(8,128)S(1)} %copy-done.1), custom_call_target="tpu_custom_call" | custom-call | tf_op jit(solution)/shard_map/columns/pallas_call | solution.py:539
  36.3 0.0 copy-start.2
  36.3 0.0 copy-start.3
  36.4 0.0 copy-start.4
  36.4 30.5 %all_to_all.11.in_ref = f32[128,24,128]{2,1,0:T(8,128)S(1)} all-to-all(f32[128,24,128]{2,1,0:T(8,128)S(1)} %columns.1), channel_id=1, replica_groups=mesh['plane'=2,'slab'=64] {'plane','slab'}, dimensions={0} | all-to-all | bytes 3145728 | tf_op jit(solution)/shard_map/all_to_all | solution.py:581
  66.9 0.0 copy-done.2
  66.9 0.0 copy-done.3
  66.9 0.0 copy-done.4
  66.9 7.4 %rays.1 = (f32[2,8,4096]{2,1,0:T(8,128)}, f32[4,8,4096]{2,1,0:T(8,128)}) custom-call(f32[128,24,128]{2,1,0:T(8,128)S(1)} %all_to_all.11.in_ref, bf16[3,128,256]{2,1,0:T(8,128)(2,1)S(1)} %copy-done.3, f32[2,32,128]{2,1,0:T(8,128)S(1)} %copy-done.4, f32[2,8,4096]{2,1,0:T(8,128)S(1)} %bitcast.9), custom_call_target="tpu_custom_call" | custom-call | tf_op jit(solution)/shard_map/rays/pallas_call | solution.py:539
Async XLA Ops:
  3.8 28.3 %copy-start = (bf16[2,3,3,128,256]{4,3,2,1,0:T(8,128)(2,1)S(1)}, bf16[2,3,3,128,256]{4,3,2,1,0:T(8,128)(2,1)}, u32[]{:S(2)}) copy-start(bf16[2,3,3,128,256]{4,3,2,1,0:T(8,128)(2,1)} %constant.21.clone.inv_ref) | copy-start | bytes 3538948
  3.8 28.3 %copy-start.1 = (f32[2,3,2,64,128]{4,3,2,1,0:T(8,128)S(1)}, f32[2,3,2,64,128]{4,3,2,1,0:T(8,128)}, u32[]{:S(2)}) copy-start(f32[2,3,2,64,128]{4,3,2,1,0:T(8,128)} %constant.22.clone.back_ref) | copy-start | bytes 1179652
  3.8 28.3 %copy-start.5 = (bf16[256,256]{1,0:T(8,128)(2,1)S(1)}, bf16[256,256]{1,0:T(8,128)(2,1)}, u32[]{:S(2)}) copy-start(bf16[256,256]{1,0:T(8,128)(2,1)} %constant.18.clone.fwd_ref) | copy-start | bytes 393220
  3.8 28.3 %copy-start.6 = (f32[2,64,128]{2,1,0:T(8,128)S(1)}, f32[2,64,128]{2,1,0:T(8,128)}, u32[]{:S(2)}) copy-start(f32[2,64,128]{2,1,0:T(8,128)} %constant.19.clone.turn_ref) | copy-start | bytes 196612
  3.8 28.3 %copy-start.7 = (f32[64,128]{1,0:T(8,128)S(1)}, f32[64,128]{1,0:T(8,128)}, u32[]{:S(2)}) copy-start(f32[64,128]{1,0:T(8,128)} %constant.20.clone.wave_ref) | copy-start | bytes 98308
  36.3 30.5 %copy-start.2 = (f32[2,1,1,8,4096]{4,3,2,1,0:T(8,128)S(1)}, f32[2,1,1,8,4096]{4,3,2,1,0:T(8,128)}, u32[]{:S(2)}) copy-start(f32[2,1,1,8,4096]{4,3,2,1,0:T(8,128)} %param.11) | copy-start | bytes 786436
  36.3 30.5 %copy-start.3 = (bf16[3,128,256]{2,1,0:T(8,128)(2,1)S(1)}, bf16[3,128,256]{2,1,0:T(8,128)(2,1)}, u32[]{:S(2)}) copy-start(bf16[3,128,256]{2,1,0:T(8,128)(2,1)} %constant.23.clone.inv_ref) | copy-start | bytes 589828
  36.4 30.5 %copy-start.4 = (f32[2,32,128]{2,1,0:T(8,128)S(1)}, f32[2,32,128]{2,1,0:T(8,128)}, u32[]{:S(2)}) copy-start(f32[2,32,128]{2,1,0:T(8,128)} %constant.17.clone.turn_hbm.turn_ref) | copy-start | bytes 98308

commit v7 on v6

--- a/solution.py
+++ b/solution.py
@@ -400,7 +400,7 @@
                     odd[spot(t), :] = jnp.where(lane < 96, moved[t], moved[(t + 1) % OUTER])
             return carry
 
-        lax.fori_loop(0, win // 8, finish, 0, unroll=5 if q == 0 else 3)
+        lax.fori_loop(0, win // 8, finish, 0, unroll=win // 8)
 
     low_half = lane < 64
 

time: 74.5 us -> 74.1 us (level)
  no operation moved by 1% of the time
where the time goes in v7:
time: 74.1 us; the launch traced here: 73.8 us
  blocking collectives  58.7 us (79%)
  Pallas kernels  14.3 us (19%)
    all_to_all x1, blocking collectives, on_device(): lax.all_to_all(strips, ('plane', 'slab'), split_axis=0, concat_axis=0, ti...  30.5 us
    all_to_all x1, blocking collectives, on_device(): lax.all_to_all(spectra.reshape(SLABS, 32, 128), 'slab', split_axis=0, con...  28.3 us
    pallas_call x3, Pallas kernels, call(): pl.pallas_call(kernel, name=name, out_shape=outs, in_specs=[pl.BlockSpec(...  14.3 us

profile of v7, /device:TPU:1, one launch (start us, length us, event | category | flops | bytes accessed | tf_op | source)
XLA Modules:
  0.0 73.8 jit_solution(4108978024177323552)
XLA Ops:
  0.6 3.1 %rows.1 = f32[2048,128]{1,0:T(8,128)} custom-call(f32[64,4096]{1,0:T(8,128)} %bitcast.11, bf16[256,256]{1,0:T(8,128)(2,1)} %constant.16.clone.weight_hbm, f32[2,32,128]{2,1,0:T(8,128)} %constant.17.clone.turn_hbm.turn_ref), custom_call_target="tpu_custom_call" | custom-call | tf_op jit(solution)/shard_map/rows/pallas_call | solution.py:539
  3.8 0.0 copy-start
  3.8 0.0 copy-start.1
  3.8 0.0 copy-start.5
  3.8 0.0 copy-start.6
  3.8 0.0 copy-start.7
  3.8 28.3 %all_to_all.10.in_ref = f32[64,32,128]{2,1,0:T(8,128)S(1)} all-to-all(f32[64,32,128]{2,1,0:T(8,128)} %bitcast.10), channel_id=1, replica_groups=mesh['plane'=2,'slab'=64] {'slab'}, dimensions={0} | all-to-all | bytes 2097152 | tf_op jit(solution)/shard_map/all_to_all | solution.py:573
  32.1 0.0 copy-done
  32.1 0.0 copy-done.1
  32.1 0.0 copy-done.5
  32.1 0.0 copy-done.6
  32.1 0.0 copy-done.7
  32.1 4.2 %columns.1 = f32[128,24,128]{2,1,0:T(8,128)S(1)} custom-call(f32[64,32,128]{2,1,0:T(8,128)S(1)} %all_to_all.10.in_ref, bf16[256,256]{1,0:T(8,128)(2,1)S(1)} %copy-done.5, f32[2,64,128]{2,1,0:T(8,128)S(1)} %copy-done.6, f32[64,128]{1,0:T(8,128)S(1)} %copy-done.7, bf16[2,3,3,128,256]{4,3,2,1,0:T(8,128)(2,1)S(1)} %copy-done, f32[2,3,2,64,128]{4,3,2,1,0:T(8,128)S(1)} %copy-done.1), custom_call_target="tpu_custom_call" | custom-call | tf_op jit(solution)/shard_map/columns/pallas_call | solution.py:539
  36.3 0.0 copy-start.2
  36.3 0.0 copy-start.3
  36.4 0.0 copy-start.4
  36.4 30.5 %all_to_all.11.in_ref = f32[128,24,128]{2,1,0:T(8,128)S(1)} all-to-all(f32[128,24,128]{2,1,0:T(8,128)S(1)} %columns.1), channel_id=1, replica_groups=mesh['plane'=2,'slab'=64] {'plane','slab'}, dimensions={0} | all-to-all | bytes 3145728 | tf_op jit(solution)/shard_map/all_to_all | solution.py:581
  66.9 0.0 copy-done.2
  66.9 0.0 copy-done.3
  66.9 0.0 copy-done.4
  66.9 7.0 %rays.1 = (f32[2,8,4096]{2,1,0:T(8,128)}, f32[4,8,4096]{2,1,0:T(8,128)}) custom-call(f32[128,24,128]{2,1,0:T(8,128)S(1)} %all_to_all.11.in_ref, bf16[3,128,256]{2,1,0:T(8,128)(2,1)S(1)} %copy-done.3, f32[2,32,128]{2,1,0:T(8,128)S(1)} %copy-done.4, f32[2,8,4096]{2,1,0:T(8,128)S(1)} %bitcast.9), custom_call_target="tpu_custom_call" | custom-call | tf_op jit(solution)/shard_map/rays/pallas_call | solution.py:539
Async XLA Ops:
  3.8 28.3 %copy-start = (bf16[2,3,3,128,256]{4,3,2,1,0:T(8,128)(2,1)S(1)}, bf16[2,3,3,128,256]{4,3,2,1,0:T(8,128)(2,1)}, u32[]{:S(2)}) copy-start(bf16[2,3,3,128,256]{4,3,2,1,0:T(8,128)(2,1)} %constant.21.clone.inv_ref) | copy-start | bytes 3538948
  3.8 28.3 %copy-start.1 = (f32[2,3,2,64,128]{4,3,2,1,0:T(8,128)S(1)}, f32[2,3,2,64,128]{4,3,2,1,0:T(8,128)}, u32[]{:S(2)}) copy-start(f32[2,3,2,64,128]{4,3,2,1,0:T(8,128)} %constant.22.clone.back_ref) | copy-start | bytes 1179652
  3.8 28.3 %copy-start.5 = (bf16[256,256]{1,0:T(8,128)(2,1)S(1)}, bf16[256,256]{1,0:T(8,128)(2,1)}, u32[]{:S(2)}) copy-start(bf16[256,256]{1,0:T(8,128)(2,1)} %constant.18.clone.fwd_ref) | copy-start | bytes 393220
  3.8 28.3 %copy-start.6 = (f32[2,64,128]{2,1,0:T(8,128)S(1)}, f32[2,64,128]{2,1,0:T(8,128)}, u32[]{:S(2)}) copy-start(f32[2,64,128]{2,1,0:T(8,128)} %constant.19.clone.turn_ref) | copy-start | bytes 196612
  3.8 28.3 %copy-start.7 = (f32[64,128]{1,0:T(8,128)S(1)}, f32[64,128]{1,0:T(8,128)}, u32[]{:S(2)}) copy-start(f32[64,128]{1,0:T(8,128)} %constant.20.clone.wave_ref) | copy-start | bytes 98308
  36.3 30.5 %copy-start.2 = (f32[2,1,1,8,4096]{4,3,2,1,0:T(8,128)S(1)}, f32[2,1,1,8,4096]{4,3,2,1,0:T(8,128)}, u32[]{:S(2)}) copy-start(f32[2,1,1,8,4096]{4,3,2,1,0:T(8,128)} %param.11) | copy-start | bytes 786436
  36.3 30.5 %copy-start.3 = (bf16[3,128,256]{2,1,0:T(8,128)(2,1)S(1)}, bf16[3,128,256]{2,1,0:T(8,128)(2,1)}, u32[]{:S(2)}) copy-start(bf16[3,128,256]{2,1,0:T(8,128)(2,1)} %constant.23.clone.inv_ref) | copy-start | bytes 589828
  36.4 30.5 %copy-start.4 = (f32[2,32,128]{2,1,0:T(8,128)S(1)}, f32[2,32,128]{2,1,0:T(8,128)}, u32[]{:S(2)}) copy-start(f32[2,32,128]{2,1,0:T(8,128)} %constant.17.clone.turn_hbm.turn_ref) | copy-start | bytes 98308
